TPU v7x, 32 devices: a whole 2x2x4 slice. The times are simulated.
32 devices in a mesh: fsdp: 4 (over x, core), tok: 8 (over z, y).
Axes of the slice: x: 2, y: 2, z: 4, core: 2. Of those that a mesh axis runs over, the one named last changes fastest.
Arguments:
- states: bfloat16 [4, 512, 1024], P('fsdp', 'tok'), may hold values from -8 to 8
- cache_keys: bfloat16 [4, 1024, 1024], P('fsdp', 'tok'), may hold values from -6 to 6
- cache_values: bfloat16 [4, 1024, 1024], P('fsdp', 'tok'), may hold values from -6 to 6
- cache_len: int32 [4], P('fsdp'), may hold values from 1 to 1024, as said below
- token_slot: int32 [4, 512], P('fsdp', 'tok'), may hold values from 0 to 511, as said below
- bucket_table: int32 [1536], replicated, may hold values from 0 to 31
- rel_bias: float32 [32, 16], replicated, may hold values from -3 to 250
- norm_gain: float32 [1024], replicated, may hold values from 0.5 to 1.5
- w_query: bfloat16 [1024, 1024], P(('fsdp', 'tok')), may hold values from -0.0234375 to 0.0234375
- w_key: bfloat16 [1024, 1024], P(('fsdp', 'tok')), may hold values from -0.1875 to 0.1875
- w_value: bfloat16 [1024, 1024], P(('fsdp', 'tok')), may hold values from -0.1875 to 0.1875
- w_out: bfloat16 [1024, 1024], P(('fsdp', 'tok')), may hold values from -1.5 to 1.5
Outputs:
- hidden_out: bfloat16 [4, 512, 1024], P('fsdp', 'tok')
- new_keys: bfloat16 [4, 512, 1024], P('fsdp', 'tok')
- new_values: bfloat16 [4, 512, 1024], P('fsdp', 'tok')
Inputs may be any that keep to these rules, and one draw needn't show every extreme that they name: `cache_len`: one request has exactly 1024 live rows. `token_slot`: each row is a permutation of 0 to 511; every aligned block of 64 tokens of a request has exactly 8 of its slots in each aligned block of 64 slots.
All inputs are finite; a program needn't handle non-finite values.
Results may differ from a plain program's by a relative error of at most 0.0095.
Values may be sent and summed in bfloat16 or wider, within the bound.
No kernel may reach another device: no remote copies, remote signals or barrier semaphores. Data moves between devices by JAX's collectives and lax.ppermute only.
A program may use at most 64 MiB of HBM per device.

v0:
```python
import jax
import jax.numpy as jnp
from jax import lax
from jax.sharding import PartitionSpec as P

far_away = 1073741824
neg_floor = -1e30


def bias_scores(bucket_ids, bias_parts):
    bucket_count = bias_parts[0].shape[0]
    one_hot = (bucket_ids[..., None] == jnp.arange(bucket_count, dtype=jnp.int32)).astype(
        jnp.bfloat16
    )
    high_part = jnp.einsum(
        "qkb,bh->hqk", one_hot, bias_parts[0], preferred_element_type=jnp.float32
    )
    middle = jnp.einsum("qkb,bh->hqk", one_hot, bias_parts[1], preferred_element_type=jnp.float32)
    low_part = jnp.einsum("qkb,bh->hqk", one_hot, bias_parts[2], preferred_element_type=jnp.float32)
    return high_part + middle + low_part


def absorb(running, queries, query_pos, keys_here, values_here, key_pos, bucket_table, bias_parts):
    totals, peak_old, masses = running
    head_count = queries.shape[1]
    keys_split = keys_here.reshape(keys_here.shape[0], head_count, -1)
    values_split = values_here.reshape(values_here.shape[0], head_count, -1)
    scores = jnp.einsum("qhd,khd->hqk", queries, keys_split, preferred_element_type=jnp.float32)
    distance = query_pos[:, None] - key_pos[None, :]
    allowed = (distance >= 0)[None]
    bucket_ids = jnp.take(bucket_table, jnp.clip(distance, 0, bucket_table.shape[0] - 1), axis=0)
    scores = scores + bias_scores(bucket_ids, bias_parts)
    new_peak = jnp.maximum(peak_old, jnp.max(jnp.where(allowed, scores, neg_floor), axis=-1))
    weights = jnp.where(allowed, jnp.exp(scores - new_peak[..., None]), 0.0)
    shrink = jnp.exp(peak_old - new_peak)
    masses = masses * shrink + jnp.sum(weights, axis=-1)
    totals = totals * jnp.transpose(shrink)[..., None] + jnp.einsum(
        "hqk,khd->qhd",
        weights.astype(jnp.bfloat16),
        values_split,
        preferred_element_type=jnp.float32,
    )
    return (totals, new_peak, masses)


def permute_rows(selector, rows):
    return jnp.dot(selector.astype(jnp.bfloat16), rows, preferred_element_type=jnp.float32).astype(
        jnp.bfloat16
    )


def permute_ints(selector, values):
    return jnp.sum(jnp.where(selector, values[None, :], 0), axis=1).astype(jnp.int32)


def shards(
    states,
    cache_keys,
    cache_values,
    cache_len,
    token_slot,
    bucket_table,
    rel_bias,
    norm_gain,
    w_query,
    w_key,
    w_value,
    w_out,
):
    peer_count = lax.axis_size("tok")
    my_index = lax.axis_index("tok")
    tokens = states[0]
    tok_rows = tokens.shape[0]
    feature_count = tokens.shape[1]
    per_peer = tok_rows // peer_count
    head_count = rel_bias.shape[1]
    head_size = feature_count // head_count
    slot_ids = token_slot[0]
    length = cache_len[0]
    row_iota = jnp.arange(tok_rows, dtype=jnp.int32)
    ranking = jnp.sum((slot_ids[None, :] < slot_ids[:, None]).astype(jnp.int32), axis=1)
    sort_sel = ranking[None, :] == row_iota[:, None]
    sent_rows = permute_rows(sort_sel, tokens).reshape(peer_count, per_peer, feature_count)
    sent_slots = permute_ints(sort_sel, slot_ids).reshape(peer_count, per_peer)
    sent_pos = (my_index * tok_rows + permute_ints(sort_sel, row_iota)).reshape(
        peer_count, per_peer
    )
    got_rows, got_slots, got_pos = (
        lax.all_to_all(sent_rows, "tok", split_axis=0, concat_axis=0, tiled=True),
        lax.all_to_all(sent_slots, "tok", split_axis=0, concat_axis=0, tiled=True),
        lax.all_to_all(sent_pos, "tok", split_axis=0, concat_axis=0, tiled=True),
    )
    local_slot = got_slots.reshape(tok_rows) - my_index * tok_rows
    place_sel = local_slot[None, :] == row_iota[:, None]
    dealt = permute_rows(place_sel, got_rows.reshape(tok_rows, feature_count))
    dealt_pos = permute_ints(place_sel, got_pos.reshape(tok_rows))
    query_w, key_w, value_w, out_w = (
        lax.all_gather(w_query, ("fsdp", "tok"), axis=0, tiled=True),
        lax.all_gather(w_key, ("fsdp", "tok"), axis=0, tiled=True),
        lax.all_gather(w_value, ("fsdp", "tok"), axis=0, tiled=True),
        lax.all_gather(w_out, ("fsdp", "tok"), axis=0, tiled=True),
    )
    wide_in = dealt.astype(jnp.float32)
    inverse = lax.rsqrt(jnp.mean(wide_in * wide_in, axis=-1, keepdims=True) + 1e-06)
    normed = (wide_in * inverse * norm_gain).astype(jnp.bfloat16)
    queries = jnp.dot(normed, query_w, preferred_element_type=jnp.float32).astype(jnp.bfloat16)
    new_keys = jnp.dot(normed, key_w, preferred_element_type=jnp.float32).astype(jnp.bfloat16)
    new_values = jnp.dot(normed, value_w, preferred_element_type=jnp.float32).astype(jnp.bfloat16)
    query_pos = length + dealt_pos
    cache_rows = cache_keys.shape[1]
    cache_spot = my_index * cache_rows + jnp.arange(cache_rows, dtype=jnp.int32)
    key_pos = jnp.concatenate([jnp.where(cache_spot < length, cache_spot, far_away), query_pos])
    keys_here = jnp.concatenate([cache_keys[0], new_keys])
    values_here = jnp.concatenate([cache_values[0], new_values])
    bias_high = rel_bias.astype(jnp.bfloat16)
    remainder = rel_bias - bias_high.astype(jnp.float32)
    bias_middle = remainder.astype(jnp.bfloat16)
    bias_low = (remainder - bias_middle.astype(jnp.float32)).astype(jnp.bfloat16)
    bias_parts = (bias_high, bias_middle, bias_low)
    query_heads = queries.reshape(tok_rows, head_count, head_size)
    shard_len = keys_here.shape[0]
    initial = (
        jnp.zeros((tok_rows, head_count, head_size), jnp.float32),
        jnp.full((head_count, tok_rows), neg_floor, jnp.float32),
        jnp.zeros((head_count, tok_rows), jnp.float32),
    )
    running = initial
    part_keys = lax.all_gather(keys_here, "tok", axis=0, tiled=True)
    part_values = lax.all_gather(values_here, "tok", axis=0, tiled=True)
    part_pos = lax.all_gather(key_pos, "tok", axis=0, tiled=True)
    rows_in = part_keys.shape[0]
    block_len = 2 * shard_len
    shard_count = rows_in // block_len
    blocks = (
        part_keys.reshape(shard_count, block_len, feature_count),
        part_values.reshape(shard_count, block_len, feature_count),
        part_pos.reshape(shard_count, block_len),
    )

    def advance(running_in, block_set):
        return (
            absorb(
                running_in,
                query_heads,
                query_pos,
                block_set[0],
                block_set[1],
                block_set[2],
                bucket_table,
                bias_parts,
            ),
            None,
        )

    running, unused = lax.scan(advance, running, blocks)
    totals, peaks, masses = running
    context = (
        (totals / jnp.transpose(masses)[..., None])
        .reshape(tok_rows, feature_count)
        .astype(jnp.bfloat16)
    )
    result_dealt = (wide_in + jnp.dot(context, out_w, preferred_element_type=jnp.float32)).astype(
        jnp.bfloat16
    )
    back_rows = permute_rows(jnp.transpose(place_sel), result_dealt).reshape(
        peer_count, per_peer, feature_count
    )
    returned = lax.all_to_all(back_rows, "tok", split_axis=0, concat_axis=0, tiled=True)
    hidden = permute_rows(jnp.transpose(sort_sel), returned.reshape(tok_rows, feature_count))
    return (hidden[None], new_keys[None], new_values[None])


def solution(mesh):
    in_specs = (
        P("fsdp", "tok", None),
        P("fsdp", "tok", None),
        P("fsdp", "tok", None),
        P("fsdp"),
        P("fsdp", "tok"),
        P(),
        P(),
        P(),
        P(("fsdp", "tok"), None),
        P(("fsdp", "tok"), None),
        P(("fsdp", "tok"), None),
        P(("fsdp", "tok"), None),
    )
    out_specs = (P("fsdp", "tok", None), P("fsdp", "tok", None), P("fsdp", "tok", None))
    return jax.shard_map(shards, mesh=mesh, in_specs=in_specs, out_specs=out_specs, check_vma=False)
```

profile of v0, /device:TPU:0, one launch (start us, length us, event | category | flops | bytes accessed | tf_op | source)
XLA Modules:
  0.0 936.9 jit_solution(472488924100509051)
XLA Ops:
  9.4 0.9 convert_reduce_fusion
  11.8 7.3 all-to-all-start
  19.9 5.6 all-to-all-done
  25.4 3.4 all-to-all-start.1
  29.0 7.2 all-to-all-done.1
  38.0 32.8 %all-gather.13.cloned.1.call-done = bf16[1024,1024]{1,0:T(8,128)(2,1)} async-done(((bf16[32,1024]{1,0:T(8,128)(2,1)}), bf16[1024,1024]{1,0:T(8,128)(2,1)}) %all-gather.13.cloned.1.call-update) | async-done | bytes 2097168 | tf_op jit(solution)/shard_map/all_gather | solution.py:100
  70.8 2.1 convolution_convert_fusion.2
  74.4 54.8 %all-gather.7.cloned.1.call-done = bf16[1024,1024]{1,0:T(8,128)(2,1)} async-done(((bf16[32,1024]{1,0:T(8,128)(2,1)}), bf16[1024,1024]{1,0:T(8,128)(2,1)}) %all-gather.7.cloned.1.call-update) | async-done | bytes 2097168 | tf_op jit(solution)/shard_map/all_gather | solution.py:99
  129.2 2.1 convolution_convert_fusion.4
  133.4 4.4 all-to-all-start.2
  140.4 3.7 all-to-all-done.2
  145.7 8.7 all-reduce
  154.4 33.1 %all-gather.11.cloned.1.call-done = bf16[1024,1024]{1,0:T(8,128)(2,1)} async-done(((bf16[32,1024]{1,0:T(8,128)(2,1)}), bf16[1024,1024]{1,0:T(8,128)(2,1)}) %all-gather.11.cloned.1.call-update) | async-done | bytes 2097168 | tf_op jit(solution)/shard_map/all_gather | solution.py:98
  187.6 2.1 convolution_convert_fusion.3
  190.6 58.3 %all-gather.15.cloned.1.call-done = bf16[1536,1024]{1,0:T(8,128)(2,1)} async-done(((bf16[192,1024]{1,0:T(8,128)(2,1)}), bf16[1536,1024]{1,0:T(8,128)(2,1)}) %all-gather.15.cloned.1.call-update) | async-done | bytes 3145744 | tf_op jit(solution)/shard_map/all_gather | solution.py:129
  249.0 61.1 %all-gather.9.cloned.1.call-done = bf16[1536,1024]{1,0:T(8,128)(2,1)} async-done(((bf16[192,1024]{1,0:T(8,128)(2,1)}), bf16[1536,1024]{1,0:T(8,128)(2,1)}) %all-gather.9.cloned.1.call-update) | async-done | bytes 3145744 | tf_op jit(solution)/shard_map/all_gather | solution.py:128
  310.1 605.3 %while.15 = (s32[]{:T(128)}, f32[64,16,64]{0,2,1:T(8,128)}, f32[16,64]{1,0:T(8,128)S(1)}, f32[16,64]{1,0:T(8,128)S(1)}, s32[64]{0:T(128)S(1)}, /*index=5*/s32[4,...) while((s32[]{:T(128)}, f32[64,16,64]{0,2,1:T(8,128)}, ...), condition=%wide.region_8.9_spmd.clone, body=%wide.region_5.8_spmd.clone.sunk | while | flops 183465984 | bytes 27471288 | solution.py:155
  310.3 135.5 %gather_fusion = s32[24576]{0:T(1024)S(1)} fusion(s32[1536]{0:T(1024)S(1)} %get-tuple-element.335, s32[24576]{0:T(1024)S(1)} %broadcast_clamp_fusion.2), kind=kCustom, calls=%fused_computation.clone.clone.1 | custom fusion | bytes 294912 | tf_op jit(solution)/shard_map/while/body/eval_jaxpr/jit(_take)/gather | solution.py:31
  446.5 1.8 fusion.71
  448.3 1.7 fusion.72
  450.1 2.4 constant_dynamic-slice_fusion.3
  452.5 1.2 copy.53
  453.7 4.1 select_reduce_fusion.5
  459.3 1.3 fusion.74
  460.8 135.5 %gather_fusion = s32[24576]{0:T(1024)S(1)} fusion(s32[1536]{0:T(1024)S(1)} %get-tuple-element.335, s32[24576]{0:T(1024)S(1)} %broadcast_clamp_fusion.2), kind=kCustom, calls=%fused_computation.clone.clone.1 | custom fusion | bytes 294912 | tf_op jit(solution)/shard_map/while/body/eval_jaxpr/jit(_take)/gather | solution.py:31
  597.1 1.8 fusion.71
  598.9 1.7 fusion.72
  600.7 2.4 constant_dynamic-slice_fusion.3
  603.1 1.2 copy.53
  604.2 4.1 select_reduce_fusion.5
  609.8 2.4 fusion.74
  612.4 135.5 %gather_fusion = s32[24576]{0:T(1024)S(1)} fusion(s32[1536]{0:T(1024)S(1)} %get-tuple-element.335, s32[24576]{0:T(1024)S(1)} %broadcast_clamp_fusion.2), kind=kCustom, calls=%fused_computation.clone.clone.1 | custom fusion | bytes 294912 | tf_op jit(solution)/shard_map/while/body/eval_jaxpr/jit(_take)/gather | solution.py:31
  748.7 1.8 fusion.71
  750.4 1.7 fusion.72
  752.3 2.4 constant_dynamic-slice_fusion.3
  754.6 1.2 copy.53
  755.8 4.1 select_reduce_fusion.5
  761.4 2.4 fusion.74
  764.0 135.5 %gather_fusion = s32[24576]{0:T(1024)S(1)} fusion(s32[1536]{0:T(1024)S(1)} %get-tuple-element.335, s32[24576]{0:T(1024)S(1)} %broadcast_clamp_fusion.2), kind=kCustom, calls=%fused_computation.clone.clone.1 | custom fusion | bytes 294912 | tf_op jit(solution)/shard_map/while/body/eval_jaxpr/jit(_take)/gather | solution.py:31
  900.3 1.8 fusion.71
  902.0 1.7 fusion.72
  903.9 2.4 constant_dynamic-slice_fusion.3
  906.2 1.2 copy.53
  907.4 4.1 select_reduce_fusion.5
  913.0 2.4 fusion.74
  915.4 1.1 divide_convert_fusion
  916.6 2.2 fusion.25
  918.8 10.4 %all_to_all.25 = bf16[8,8,1024]{2,1,0:T(8,128)(2,1)S(1)} all-to-all(bf16[8,8,1024]{2,1,0:T(8,128)(2,1)S(1)} %fusion.25), channel_id=1, replica_groups=mesh['fsdp'=4,'tok'=8] {'tok'}, dimensions={0} | all-to-all | bytes 262144 | tf_op jit(solution)/shard_map/all_to_all | solution.py:168
  (128 shorter events, 24.2 us)
Async XLA Ops:
  7.2 11.9 %copy-start = (bf16[1,64,1024]{2,1,0:T(8,128)(2,1)S(1)}, bf16[1,64,1024]{2,1,0:T(8,128)(2,1)}, u32[]{:S(2)}) copy-start(bf16[1,64,1024]{2,1,0:T(8,128)(2,1)} %param.14) | copy-start | bytes 393220
  7.2 63.6 %all-gather.13.cloned.1.call-start = ((), (), s32[]{:S(2)}) async-start(), calls=%async_computation.7 | async-start | bytes 2162688 | tf_op jit(solution)/shard_map/all_gather | solution.py:100
  7.9 121.3 %all-gather.7.cloned.1.call-start = ((), (), s32[]{:S(2)}) async-start(), calls=%async_computation.4 | async-start | bytes 2162688 | tf_op jit(solution)/shard_map/all_gather | solution.py:99
  8.7 178.9 %all-gather.11.cloned.1.call-start = ((), (), s32[]{:S(2)}) async-start(), calls=%async_computation.6 | async-start | bytes 2162688 | tf_op jit(solution)/shard_map/all_gather | solution.py:98
  10.3 15.1 %copy-start.11 = (s32[64]{0:T(128)}, s32[64]{0:T(128)S(1)}, u32[]{:S(2)}) copy-start(s32[64]{0:T(128)S(1)} %convert_reduce_fusion) | copy-start | bytes 772
  11.8 13.7 %all-to-all-start = ((s32[8,1,8]{2,1,0:T(1,128)}), s32[8,1,8]{2,1,0:T(1,128)S(1)}, u32[]{:S(2)}, u32[]{:S(2)}) async-start(s32[8,1,8]{2,1,0:T(1,128)} %bitcast.1), calls=%async_computation | async-start | bytes 8192 | tf_op jit(solution)/shard_map/all_to_all | solution.py:90
  25.4 10.8 %all-to-all-start.1 = ((bf16[8,8,1024]{2,1,0:T(8,128)(2,1)}), bf16[8,8,1024]{2,1,0:T(8,128)(2,1)S(1)}, u32[]{:S(2)}, u32[]{:S(2)}) async-start(bf16[8,8,1024]{2,1,0:T(8,128)(2,1)} %fusion.26), calls=%async_computation.1 | async-start | bytes 262144 | tf_op jit(solution)/shard_map/all_to_all | solution.py:89
  28.8 220.1 %all-gather.15.cloned.1.call-start = ((), (), s32[]{:S(2)}) async-start(), calls=%async_computation.8 | async-start | bytes 3538944 | tf_op jit(solution)/shard_map/all_gather | solution.py:129
  29.0 116.4 %copy-start.9 = (s32[64]{0:T(128)}, s32[64]{0:T(128)S(1)}, u32[]{:S(2)}) copy-start(s32[64]{0:T(128)S(1)} %sub.69) | copy-start | bytes 772
  29.0 44.5 %copy-start.6 = (bf16[1,128,1024]{2,1,0:T(8,128)(2,1)S(1)}, bf16[1,128,1024]{2,1,0:T(8,128)(2,1)}, u32[]{:S(2)}) copy-start(bf16[1,128,1024]{2,1,0:T(8,128)(2,1)} %param.16) | copy-start | bytes 786436
  36.5 0.7 copy-start.3
  72.9 0.7 copy-start.4
  74.3 57.6 %copy-start.7 = (bf16[1,128,1024]{2,1,0:T(8,128)(2,1)S(1)}, bf16[1,128,1024]{2,1,0:T(8,128)(2,1)}, u32[]{:S(2)}) copy-start(bf16[1,128,1024]{2,1,0:T(8,128)(2,1)} %param.15) | copy-start | bytes 786436
  74.3 64.7 %copy-start.8 = (f32[32,16]{0,1:T(8,128)S(1)}, f32[32,16]{0,1:T(8,128)}, u32[]{:S(2)}) copy-start(f32[32,16]{0,1:T(8,128)} %param.20) | copy-start | bytes 6148
  74.3 64.7 %copy-start.13 = (u32[32]{0:T(128)S(1)}, u32[32]{0:T(128)}, u32[]{:S(2)}) copy-start(u32[32]{0:T(128)} %constant.64) | copy-start | bytes 388
  74.4 235.7 %all-gather.9.cloned.1.call-start = ((), (), s32[]{:S(2)}) async-start(), calls=%async_computation.5 | async-start | bytes 3538944 | tf_op jit(solution)/shard_map/all_gather | solution.py:128
  131.3 0.7 copy-start.5
  133.4 10.8 %all-to-all-start.2 = ((s32[8,1,8]{2,1,0:T(1,128)}), s32[8,1,8]{2,1,0:T(1,128)S(1)}, u32[]{:S(2)}, u32[]{:S(2)}) async-start(s32[8,1,8]{2,1,0:T(1,128)} %bitcast.6), calls=%async_computation.2 | async-start | bytes 8192 | tf_op jit(solution)/shard_map/all_to_all | solution.py:91
  137.8 778.8 %all-gather.17.cloned.1.call-start = ((), (), s32[]{:S(2)}) async-start(), calls=%async_computation.9 | async-start | bytes 2162688 | tf_op jit(solution)/shard_map/all_gather | solution.py:101
  154.4 155.7 %copy-start.1 = (s32[1536]{0:T(1024)S(1)}, s32[1536]{0:T(1024)}, u32[]{:S(2)}) copy-start(s32[1536]{0:T(1024)} %param.19) | copy-start | bytes 18436
  310.1 606.5 %copy-start.10 = (s32[64]{0:T(128)S(1)}, s32[64]{0:T(128)}, u32[]{:S(2)}) copy-start(s32[64]{0:T(128)} %copy-done.9) | copy-start | bytes 772
  457.8 1.2 copy-start.2
  608.3 1.2 copy-start.2
  759.9 1.2 copy-start.2
  911.5 1.2 copy-start.2
  916.5 12.7 %copy-start.12 = (s32[64]{0:T(128)S(1)}, s32[64]{0:T(128)}, u32[]{:S(2)}) copy-start(s32[64]{0:T(128)} %copy-done.11) | copy-start | bytes 772
Sparse Core Ops, SparseCore 0:
  11.0 59.7 all-gather.12
  73.8 55.3 all-gather.6
  132.2 55.3 all-gather.10
  189.6 59.2 all-gather.14
  251.0 59.0 all-gather.8
  312.9 55.1 all-gather.16
where the time goes:
time: 938 us; the launch traced here: 937 us
  local copies, waits for them, and re-layouts  566 us (60%)
  waiting for transfers between devices  259 us (28%)
  matrix products  51.5 us (5%)
  blocking collectives  19.1 us (2%)
  between operations  15.7 us (2%)
  starting transfers between devices  15.2 us (2%)
  other arithmetic  9.68 us (1%)
    gather x8, local copies, waits for them, and re-layouts, absorb(): jnp.take(bucket_table, jnp.clip(distance, 0, bucket_table.shape[0] - 1),...  542 us
    all_gather x1, waiting for transfers between devices, shards(): part_keys = lax.all_gather(keys_here, 'tok', axis=0, tiled=True)  61.1 us
    all_gather x1, waiting for transfers between devices, shards(): part_values = lax.all_gather(values_here, 'tok', axis=0, tiled=True)  58.3 us
    all_gather x1, waiting for transfers between devices, shards(): lax.all_gather(w_key, ('fsdp', 'tok'), axis=0, tiled=True)  54.8 us
    all_gather x1, waiting for transfers between devices, shards(): lax.all_gather(w_query, ('fsdp', 'tok'), axis=0, tiled=True)  33.1 us
    all_gather x1, waiting for transfers between devices, shards(): lax.all_gather(w_value, ('fsdp', 'tok'), axis=0, tiled=True)  32.8 us
  transfers between devices with their start and end apart: 9, of which 8 were waited for; matrix products, arithmetic and copies ran while one was open for 66% of the time, Pallas kernels for 0%

commit v1 on v0

v1 whole, which is shorter than its diff:
```python
import functools

import jax
import jax.numpy as jnp
from jax import lax
from jax.experimental import pallas as pl
from jax.experimental.pallas import tpu as pltpu
from jax.sharding import PartitionSpec as P

masked = -1e30
q_rows = 128
lanes = 128
slot_base = 32
vmem_bytes = 32 * 1024 * 1024


def bias_rows(bucket_table, head_bias, new_count):
    buckets = jnp.arange(head_bias.shape[1], dtype=jnp.int32)

    def look_up(table):
        hit = table[None, None, :] == buckets[None, :, None]
        return jnp.sum(jnp.where(hit, head_bias[:, :, None], 0.0), axis=1)

    first = new_count - q_rows
    cache_order = jnp.concatenate(
        [jnp.flip(bucket_table[: first + 1]), jnp.flip(bucket_table[first + 1 :])]
    )
    new_order = jnp.concatenate(
        [
            jnp.flip(bucket_table[: first + 1]),
            jnp.full((new_count,), -1, jnp.int32),
            jnp.flip(bucket_table[first + 1 : new_count]),
        ]
    )
    new_bias = jnp.where((new_order < 0)[None], masked, look_up(new_order))
    return look_up(cache_order), new_bias


def qkv_kernel(place_ref, x_ref, w_ref, q_ref, k_ref, v_ref):
    width = q_ref.shape[1]
    count = place_ref.shape[0]
    rows = x_ref.shape[0] // count
    for part, out in enumerate((q_ref, k_ref, v_ref)):
        made = jnp.dot(
            x_ref[...],
            w_ref[:, part * width : (part + 1) * width],
            preferred_element_type=jnp.float32,
        ).astype(jnp.bfloat16)
        for block in range(count):
            spot = pl.multiple_of(place_ref[block] * rows, rows)
            out[pl.ds(spot, rows), :] = made[block * rows : (block + 1) * rows]


def table_kernel(len_ref, cache_row_ref, new_row_ref, cache_tab, new_tab):
    for row_ref, tab, shift in ((cache_row_ref, cache_tab, len_ref[0]), (new_row_ref, new_tab, None)):
        span = tab.shape[2]
        for h in range(tab.shape[0]):
            base = jnp.broadcast_to(row_ref[h : h + 1, :], (8, span))
            if shift is not None:
                base = pltpu.roll(base, shift, 1)
            row = lax.broadcasted_iota(jnp.int32, (8, span), 0)
            for bit in (1, 2, 4):
                base = jnp.where((row & bit) != 0, pltpu.roll(base, bit, 1), base)
            for group in range(tab.shape[1] // 8):
                tab[h, group * 8 : (group + 1) * 8, :] = (
                    pltpu.roll(base, group * 8, 1) if group else base
                )


def attend_kernel(
    head_count,
    head_size,
    len_ref,
    q_ref,
    k_ref,
    v_ref,
    cache_ref,
    cache_tab,
    new_tab,
    slots_ref,
    out_ref,
    key_aug,
    val_aug,
    new_val_aug,
):
    peers = out_ref.shape[0]
    tok_rows = out_ref.shape[1] // 3
    new_count = q_ref.shape[0]
    width = q_ref.shape[1]
    cache_rows = (cache_ref.shape[1] - 8) // 2
    cache_count = peers * cache_rows
    length = len_ref[0]

    old_keys = cache_ref[:, :cache_rows, :].reshape(cache_count, width)
    old_vals = cache_ref[:, cache_rows : 2 * cache_rows, :].reshape(cache_count, width)
    key_row = lax.broadcasted_iota(jnp.int32, (cache_count, width), 0)
    key_lane = lax.broadcasted_iota(jnp.int32, (cache_count, width), 1)
    new_lane = lax.broadcasted_iota(jnp.int32, (new_count, width), 1)
    dead = jnp.where(key_row < length, 0.0, masked).astype(jnp.bfloat16)
    one = jnp.ones((), jnp.bfloat16)
    for h in range(head_count):
        spare = ((h + 1) * head_size) % width
        mine = (key_lane >= h * head_size) & (key_lane < (h + 1) * head_size)
        mine_new = (new_lane >= h * head_size) & (new_lane < (h + 1) * head_size)
        key_aug[h] = jnp.where(key_lane == spare, dead, old_keys)
        val_aug[h] = jnp.where(mine, old_vals, one)
        new_val_aug[h] = jnp.where(mine_new, v_ref[...], one)

    lane = lax.broadcasted_iota(jnp.int32, (q_rows, width), 1)
    per_dest = tok_rows
    for block in range(new_count // q_rows):
        q_here = q_ref[block * q_rows : (block + 1) * q_rows, :]
        start = new_count - q_rows - block * q_rows
        seen = (block + 1) * q_rows
        made = None
        for h in range(head_count):
            spare = ((h + 1) * head_size) % width
            mine = (lane >= h * head_size) & (lane < (h + 1) * head_size)
            q_new = jnp.where(mine, q_here, jnp.zeros((), jnp.bfloat16))
            q_old = jnp.where(lane == spare, one, q_new)
            s_old = lax.dot_general(
                q_old, key_aug[h], (((1,), (1,)), ((), ())), preferred_element_type=jnp.float32
            )
            s_new = lax.dot_general(
                q_new,
                k_ref[:seen, :],
                (((1,), (1,)), ((), ())),
                preferred_element_type=jnp.float32,
            )
            s_old = s_old + cache_tab[h, :, start : start + cache_count]
            s_new = s_new + new_tab[h, :, start : start + seen]
            peak = jnp.maximum(
                jnp.max(s_old, axis=1, keepdims=True), jnp.max(s_new, axis=1, keepdims=True)
            )
            p_old = jnp.exp(s_old - peak).astype(jnp.bfloat16)
            p_new = jnp.exp(s_new - peak).astype(jnp.bfloat16)
            total = jnp.dot(p_old, val_aug[h], preferred_element_type=jnp.float32) + jnp.dot(
                p_new, new_val_aug[h, :seen, :], preferred_element_type=jnp.float32
            )
            part = total / total[:, spare : spare + 1]
            made = part if made is None else jnp.where(mine, part, made)
        made = made.astype(jnp.bfloat16)
        for piece in range(q_rows // per_dest):
            out_ref[block * (q_rows // per_dest) + piece, :per_dest, :] = made[
                piece * per_dest : (piece + 1) * per_dest
            ]

    slot_row = lax.broadcasted_iota(jnp.int32, (new_count, new_count), 0)
    deal = (slots_ref[...] == slot_row).astype(jnp.bfloat16)
    for part, ref in ((1, k_ref), (2, v_ref)):
        dealt = jnp.dot(deal, ref[...], preferred_element_type=jnp.float32).astype(jnp.bfloat16)
        for dest in range(peers):
            out_ref[dest, part * tok_rows : (part + 1) * tok_rows, :] = dealt[
                dest * tok_rows : (dest + 1) * tok_rows
            ]


def finish_kernel(got_ref, w_ref, states_ref, hidden_ref, keys_ref, values_ref):
    peers = got_ref.shape[0]
    rows = states_ref.shape[0]
    context = jnp.concatenate([got_ref[p, :rows, :] for p in range(peers)], axis=1)
    keys_ref[...] = jnp.concatenate([got_ref[p, rows : 2 * rows, :] for p in range(peers)], axis=1)
    values_ref[...] = jnp.concatenate(
        [got_ref[p, 2 * rows : 3 * rows, :] for p in range(peers)], axis=1
    )
    hidden_ref[...] = (
        states_ref[...].astype(jnp.float32)
        + jnp.dot(context, w_ref[...], preferred_element_type=jnp.float32)
    ).astype(jnp.bfloat16)


def vmem():
    return pl.BlockSpec(memory_space=pltpu.VMEM)


def smem():
    return pl.BlockSpec(memory_space=pltpu.SMEM)


def call(kernel, outs, specs, scratch, name, flops, moved, kind=jnp.bfloat16):
    return pl.pallas_call(
        kernel,
        out_shape=[jax.ShapeDtypeStruct(shape, kind) for shape in outs],
        in_specs=specs,
        out_specs=[vmem() for unused in outs],
        scratch_shapes=scratch,
        name=name,
        cost_estimate=pl.CostEstimate(flops=flops, bytes_accessed=moved, transcendentals=0),
        compiler_params=pltpu.CompilerParams(vmem_limit_bytes=vmem_bytes),
    )


def shards(
    near,
    states,
    cache_keys,
    cache_values,
    cache_len,
    token_slot,
    bucket_table,
    rel_bias,
    norm_gain,
    w_query,
    w_key,
    w_value,
    w_out,
):
    peers = lax.axis_size("tok")
    me = lax.axis_index("tok")
    tokens = states[0]
    tok_rows, features = tokens.shape
    heads = rel_bias.shape[1]
    head_size = features // heads
    width = features // peers
    my_heads = width // head_size
    new_count = tok_rows * peers
    cache_rows = cache_keys.shape[1]

    out_w = lax.all_gather(w_out, ("fsdp", "tok"), axis=0, tiled=True)

    sent_w = jnp.stack([w_query, w_key, w_value], axis=1).reshape(-1, 3, peers, width)
    sent_w = jnp.transpose(sent_w, (2, 0, 1, 3)).reshape(peers, -1, 3 * width)
    got_w = lax.all_to_all(sent_w, "tok", split_axis=0, concat_axis=0, tiled=True)
    my_w = lax.all_gather(got_w.reshape(-1, 3 * width), "fsdp", axis=0, tiled=True)

    wide_in = tokens.astype(jnp.float32)
    inverse = lax.rsqrt(jnp.mean(wide_in * wide_in, axis=-1, keepdims=True) + 1e-06)
    normed = (wide_in * inverse * norm_gain).astype(jnp.bfloat16)
    far = peers // near
    parts, place = [], []
    for step in range(far):
        pairs = [(t, (t + near * step) % peers) for t in range(peers)]
        parts.append(lax.ppermute(normed, "tok", pairs) if step else normed)
        place.append((me + peers - near * step) % peers)
    for turn in range(1, near):
        for step in range(far):
            pairs = [(t, t - t % near + (t + turn) % near) for t in range(peers)]
            parts.append(lax.ppermute(parts[step], "tok", pairs))
            origin = place[step]
            place.append(origin - origin % near + (origin + near - turn) % near)
    gathered = jnp.concatenate(parts)
    place = jnp.stack(place).astype(jnp.int32)

    def columns(rows):
        return jnp.transpose(rows.reshape(-1, peers, width), (1, 0, 2))

    slots = token_slot[0]
    note = jnp.zeros((8, width), jnp.bfloat16)
    note = note.at[0, :tok_rows].set((slots // slot_base).astype(jnp.bfloat16))
    note = note.at[1, :tok_rows].set((slots % slot_base).astype(jnp.bfloat16))
    sent_cache = jnp.concatenate(
        [
            columns(cache_keys[0]),
            columns(cache_values[0]),
            jnp.broadcast_to(note[None], (peers, 8, width)),
        ],
        axis=1,
    )
    cache = lax.all_to_all(sent_cache, "tok", split_axis=0, concat_axis=0, tiled=True)
    notes = cache[:, 2 * cache_rows : 2 * cache_rows + 2, :tok_rows].astype(jnp.int32)
    all_slots = (notes[:, 0] * slot_base + notes[:, 1]).reshape(1, new_count)

    my_bias = jnp.transpose(lax.dynamic_slice_in_dim(rel_bias, me * my_heads, my_heads, axis=1))
    cache_bias, new_bias = bias_rows(bucket_table, my_bias, new_count)

    cache_tab, new_tab = call(
        table_kernel,
        [(my_heads, q_rows, row.shape[1]) for row in (cache_bias, new_bias)],
        [smem(), vmem(), vmem()],
        [],
        "tables",
        0,
        4 * my_heads * q_rows * (cache_bias.shape[1] + new_bias.shape[1]),
        jnp.float32,
    )(cache_len, cache_bias, new_bias)

    queries, keys, values = call(
        qkv_kernel,
        [(new_count, width)] * 3,
        [smem(), vmem(), vmem()],
        [],
        "qkv",
        6 * new_count * features * width,
        2 * features * (new_count + 3 * width),
    )(place, gathered, my_w)

    if width < lanes:
        pad = ((0, 0), (0, lanes - width))
        queries, keys, values = (jnp.pad(one, pad) for one in (queries, keys, values))
        cache = jnp.pad(cache, ((0, 0),) + pad)
    full = max(width, lanes)
    (sent,) = call(
        functools.partial(attend_kernel, my_heads, head_size),
        [(peers, 3 * tok_rows, full)],
        [smem()] + [vmem()] * 7,
        [
            pltpu.VMEM((my_heads, peers * cache_rows, full), jnp.bfloat16),
            pltpu.VMEM((my_heads, peers * cache_rows, full), jnp.bfloat16),
            pltpu.VMEM((my_heads, new_count, full), jnp.bfloat16),
        ],
        "attend",
        4 * my_heads * new_count * (new_count + peers * cache_rows) * full,
        2 * full * (3 * new_count + 2 * peers * cache_rows),
    )(cache_len, queries, keys, values, cache, cache_tab, new_tab, all_slots)
    sent = sent[:, :, :width]

    got = lax.all_to_all(sent, "tok", split_axis=0, concat_axis=0, tiled=True)
    hidden, new_keys, new_values = call(
        finish_kernel,
        [(tok_rows, features)] * 3,
        [vmem()] * 3,
        [],
        "finish",
        2 * tok_rows * features * features,
        2 * features * (features + 5 * tok_rows),
    )(got, out_w, tokens)
    return (hidden[None], new_keys[None], new_values[None])


def solution(mesh):
    in_specs = (
        P("fsdp", "tok", None),
        P("fsdp", "tok", None),
        P("fsdp", "tok", None),
        P("fsdp"),
        P("fsdp", "tok"),
        P(),
        P(),
        P(),
        P(("fsdp", "tok"), None),
        P(("fsdp", "tok"), None),
        P(("fsdp", "tok"), None),
        P(("fsdp", "tok"), None),
    )
    out_specs = (P("fsdp", "tok", None), P("fsdp", "tok", None), P("fsdp", "tok", None))
    near = 2 if mesh.shape["tok"] <= 8 else 4
    return jax.shard_map(
        functools.partial(shards, near),
        mesh=mesh,
        in_specs=in_specs,
        out_specs=out_specs,
        check_vma=False,
    )
```

time: 938 us -> 102 us (0.11)
  local copies, waits for them, and re-layouts: 566 us -> 14.5 us
  waiting for transfers between devices: 259 us -> 2.57 us
  matrix products: 51.5 us -> 0 us
  blocking collectives: 19.1 us -> 34 us
    gather x8 -> x0, local copies, waits for them, and re-layouts: 542 us -> none  [absorb(): jnp.take(bucket_table, jnp.clip(distance, 0, bucket_table.shape[0] - 1),...]
    all_gather x6 -> x1, waiting for transfers between devices: 240 us -> 0.93 us  [shards(): out_w = lax.all_gather(w_out, ('fsdp', 'tok'), axis=0, tiled=True)]
    dot_general x27 -> x0, matrix products: 51.5 us -> none  [the longest x4 16.3 us: absorb(): jnp.einsum('qhd,khd->hqk', queries, keys_split, preferred_element_type=jn...]
    all_to_all x3 -> x2, waiting for transfers between devices: 16.5 us -> 0.01 us  [the longest x1 0.01 us: shards(): lax.all_to_all(sent_w, 'tok', split_axis=0, concat_axis=0, tiled=True)]
    dynamic_slice x16 -> x0, local copies, waits for them, and re-layouts: 15.8 us -> none  [shards(): running, unused = lax.scan(advance, running, blocks)]
    all_to_all x1, blocking collectives: 10.4 us -> 25.4 us  [shards(): got = lax.all_to_all(sent, 'tok', split_axis=0, concat_axis=0, tiled=True)]
    ppermute x0 -> x7, starting transfers between devices: none -> 12.7 us  [the longest x3 6.96 us: shards(): parts.append(lax.ppermute(normed, 'tok', pairs) if step else normed)]
  transfers between devices with their start and end apart: 9 -> 10, of which waited for: 8 -> 2; matrix products, arithmetic and copies ran while one was open for 66% -> 11% of each run, Pallas kernels for 0% -> 7%
where the time goes in v1:
time: 102 us; the launch traced here: 101 us
  blocking collectives  34 us (33%)
  starting transfers between devices  22.1 us (22%)
  between operations  15.2 us (15%)
  local copies, waits for them, and re-layouts  14.5 us (14%)
  Pallas kernels  8.07 us (8%)
  other arithmetic  4.63 us (5%)
  waiting for transfers between devices  2.57 us (3%)
    all_to_all x1, blocking collectives, shards(): got = lax.all_to_all(sent, 'tok', split_axis=0, concat_axis=0, tiled=True)  25.4 us
    unnamed x39, local copies, waits for them, and re-layouts  12.4 us
    all_gather x1, blocking collectives, shards(): lax.all_gather(got_w.reshape(-1, 3 * width), 'fsdp', axis=0, tiled=True)  8.55 us
    ppermute x3, starting transfers between devices, shards(): parts.append(lax.ppermute(normed, 'tok', pairs) if step else normed)  6.96 us
    all_to_all x1, starting transfers between devices, shards(): lax.all_to_all(sent_cache, 'tok', split_axis=0, concat_axis=0, tiled=True)  5.92 us
    ppermute x4, starting transfers between devices, shards(): parts.append(lax.ppermute(parts[step], 'tok', pairs))  5.76 us
    pallas_call x1, Pallas kernels, shards(): call(functools.partial(attend_kernel, my_heads, head_size), [(peers, 3 *...  3.9 us
    all_to_all x1, starting transfers between devices, shards(): lax.all_to_all(sent_w, 'tok', split_axis=0, concat_axis=0, tiled=True)  3.39 us
  transfers between devices with their start and end apart: 10, of which 2 were waited for; matrix products, arithmetic and copies ran while one was open for 11% of the time, Pallas kernels for 7%

profile of v1, /device:TPU:0, one launch (start us, length us, event | category | flops | bytes accessed | tf_op | source)
XLA Modules:
  0.0 101.0 jit_solution(9802249127445198484)
XLA Ops:
  7.2 1.1 %fusion = f32[64]{0:T(128)S(1)} fusion(bf16[1,64,1024]{2,1,0:T(8,128)(2,1)} %param.16), kind=kLoop, calls=%fused_computation.4 | loop fusion | flops 196544 | bytes 131328 | tf_op jit(solution)/shard_map/reduce_sum | solution.py:227
  8.3 1.7 %constant_dynamic-update-slice_fusion.7 = (bf16[512,1024]{1,0:T(8,128)(2,1)S(1)}, bf16[64,1024]{1,0:T(8,128)(2,1)}) fusion(f32[1024]{0:T(1024)} %param.23, f32[64]{0:T(128)S(1)} %add_rsqrt_fusion, bf16[1,64,1024]{2,1,0:T(8,128)(2,1)} %param.16), kind=kLoop, calls=%fused_computation.18 | loop fusion | flops 262143 | bytes 397568
  10.0 3.0 %collective-permute-start = (bf16[64,1024]{1,0:T(8,128)(2,1)}, bf16[64,1024]{1,0:T(8,128)(2,1)}, u32[]{:S(2)}, u32[]{:S(2)}) collective-permute-start(bf16[64,1024]{1,0:T(8,128)(2,1)} %get-tuple-element.44), channel_id=1, source_target_pairs={{0,2},{1,3},{2,4},{3,5},{4,6},{5,7},{6,0},{7,1},{8,10},{9,11},{10,... | collective-permute-start | bytes 393224 | tf_op jit(solution)/shard_map/ppermute | solution.py:233
  13.0 2.6 %collective-permute-start.1 = (bf16[64,1024]{1,0:T(8,128)(2,1)}, bf16[64,1024]{1,0:T(8,128)(2,1)}, u32[]{:S(2)}, u32[]{:S(2)}) collective-permute-start(bf16[64,1024]{1,0:T(8,128)(2,1)} %get-tuple-element.44), channel_id=1, source_target_pairs={{0,4},{1,5},{2,6},{3,7},{4,0},{5,1},{6,2},{7,3},{8,12},{9,13},{10,... | collective-permute-start | bytes 393224 | tf_op jit(solution)/shard_map/ppermute | solution.py:233
  15.6 1.3 %collective-permute-start.2 = (bf16[64,1024]{1,0:T(8,128)(2,1)}, bf16[64,1024]{1,0:T(8,128)(2,1)S(1)}, u32[]{:S(2)}, u32[]{:S(2)}) collective-permute-start(bf16[64,1024]{1,0:T(8,128)(2,1)} %get-tuple-element.44), channel_id=1, source_target_pairs={{0,6},{1,7},{2,0},{3,1},{4,2},{5,3},{6,4},{7,5},{8,14},{9,15},{10,... | collective-permute-start | bytes 393224 | tf_op jit(solution)/shard_map/ppermute | solution.py:233
  16.9 1.5 %collective-permute-start.3 = (bf16[64,1024]{1,0:T(8,128)(2,1)}, bf16[64,1024]{1,0:T(8,128)(2,1)}, u32[]{:S(2)}, u32[]{:S(2)}) collective-permute-start(bf16[64,1024]{1,0:T(8,128)(2,1)} %get-tuple-element.44), channel_id=1, source_target_pairs={{0,1},{1,0},{2,3},{3,2},{4,5},{5,4},{6,7},{7,6},{8,9},{9,8},{10,11... | collective-permute-start | bytes 393224 | tf_op jit(solution)/shard_map/ppermute | solution.py:238
  18.4 0.8 copy.32
  19.3 0.1 copy.25
  19.4 0.9 copy.31
  20.3 0.1 copy.24
  20.4 0.1 copy.23
  20.5 0.5 maximum_bitcast_fusion
  21.0 0.9 reshape.183
  21.9 3.4 %all-to-all-start = ((bf16[8,32,384]{2,1,0:T(8,128)(2,1)}), bf16[8,32,384]{2,1,0:T(8,128)(2,1)S(1)}, u32[]{:S(2)}, u32[]{:S(2)}) async-start(bf16[8,32,384]{2,1,0:T(8,128)(2,1)} %reshape.183), calls=%async_computation | async-start | bytes 393216 | tf_op jit(solution)/shard_map/all_to_all | solution.py:223
  25.3 0.7 all-gather.2.cloned.1.call-update
  26.2 0.2 copy.28
  26.4 0.2 copy.29
  26.6 0.2 copy.26
  26.8 0.2 copy.27
  27.0 0.1 reverse
  27.1 0.1 reverse.1
  27.3 0.1 rev.15
  27.4 0.1 scatter.9
  27.8 0.1 select_reduce_fusion.1
  28.0 0.8 pad_maximum_fusion
  28.9 0.1 select_reduce_fusion.cache_row_ref
  29.8 1.5 %tables.1 = (f32[2,128,1536]{2,1,0:T(8,128)S(1)}, f32[2,128,1024]{2,1,0:T(8,128)S(1)}) custom-call(s32[1]{0:T(128)S(6)} %copy.41.len_ref, f32[2,1536]{1,0:T(2,128)S(1)} %select_reduce_fusion.cache_row_ref, f32[2,1024]{1,0:T(2,128)S(1)} %broadcast_select_fusion.new_row_ref), custom_call_target="tpu_custom_call" | custom-call | bytes 2621440 | tf_op jit(solution)/shard_map/tables/pallas_call | solution.py:266
  31.4 1.0 copy-done.3
  32.4 2.0 %collective-permute-start.4 = (bf16[64,1024]{1,0:T(8,128)(2,1)}, bf16[64,1024]{1,0:T(8,128)(2,1)}, u32[]{:S(2)}, u32[]{:S(2)}) collective-permute-start(bf16[64,1024]{1,0:T(8,128)(2,1)} %collective-permute-done), channel_id=1, source_target_pairs={{0,1},{1,0},{2,3},{3,2},{4,5},{5,4},{6,7},{7,6},{8,9},{9,8},{10,11... | collective-permute-start | bytes 393224 | tf_op jit(solution)/shard_map/ppermute | solution.py:238
  34.4 0.9 constant_dynamic-update-slice_fusion.6
  35.3 0.2 collective-permute-start.5
  35.5 5.9 %all-to-all-start.1 = ((bf16[8,264,128]{2,1,0:T(8,128)(2,1)}), bf16[8,264,128]{2,1,0:T(8,128)(2,1)S(1)}, u32[]{:S(2)}, u32[]{:S(2)}) async-start(bf16[8,264,128]{2,1,0:T(8,128)(2,1)} %pad_maximum_fusion), calls=%async_computation.1 | async-start | bytes 1081344 | tf_op jit(solution)/shard_map/all_to_all | solution.py:259
  41.5 0.9 constant_dynamic-update-slice_fusion.5
  42.4 2.1 %collective-permute-start.6 = (bf16[64,1024]{1,0:T(8,128)(2,1)S(1)}, bf16[64,1024]{1,0:T(8,128)(2,1)S(1)}, u32[]{:S(2)}, u32[]{:S(2)}) collective-permute-start(bf16[64,1024]{1,0:T(8,128)(2,1)S(1)} %collective-permute-done.2), channel_id=1, source_target_pairs={{0,1},{1,0},{2,3},{3,2},{4,5},{5,4},{6,7},{7,6},{8,9},{9,8},{10,11... | collective-permute-start | bytes 393224 | tf_op jit(solution)/shard_map/ppermute | solution.py:238
  44.5 0.9 constant_dynamic-update-slice_fusion.3
  45.4 0.9 constant_dynamic-update-slice_fusion.2
  46.3 0.9 constant_dynamic-update-slice_fusion.1
  47.3 0.9 collective-permute-done.6
  48.2 8.5 %all_gather.6.w_ref = bf16[1024,384]{1,0:T(8,128)(2,1)S(1)} all-gather(bf16[256,384]{1,0:T(8,128)(2,1)S(1)} %bitcast.43), channel_id=1, replica_groups=mesh['fsdp'=4,'tok'=8] {'fsdp'}, dimensions={0}, use_global_device_ids=true | all-gather | bytes 983040 | tf_op jit(solution)/shard_map/all_gather | solution.py:224
  56.8 1.5 %qkv.1 = (bf16[512,128]{1,0:T(8,128)(2,1)S(1)}, bf16[512,128]{1,0:T(8,128)(2,1)S(1)}, bf16[512,128]{1,0:T(8,128)(2,1)S(1)}) custom-call(s32[8]{0:T(128)S(1)} %stack.47.place_ref, bf16[512,1024]{1,0:T(8,128)(2,1)S(1)} %constant_dynamic-update-slice_fusion.x_ref, bf16[1024,384]{1,0:T(8,128)(2,1)S(1)} %all_gather.6.w_ref), custom_call_target="tpu_custom_call" | custom-call | flops 402653184 | bytes 1835008 | tf_op jit(solution)/shard_map/qkv/pallas_call | solution.py:277
  58.3 0.6 copy-done.5
  59.1 1.2 %copy-done.4 = f32[2,128,1024]{2,1,0:T(8,128)S(1)} copy-done((f32[2,128,1024]{2,1,0:T(8,128)S(1)}, f32[2,128,1024]{2,1,0:T(8,128)}, u32[]{:S(2)}) %copy-start.4) | copy-done | bytes 1048600
  60.3 0.9 copy-done.6
  61.2 3.9 %attend.1 = bf16[8,192,128]{2,1,0:T(8,128)(2,1)S(1)} custom-call(s32[1]{0:T(128)S(6)} %copy.41.len_ref, bf16[512,128]{1,0:T(8,128)(2,1)S(1)} %get-tuple-element.35.q_ref, bf16[512,128]{1,0:T(8,128)(2,1)S(1)} %get-tuple-element.36.k_ref, bf16[512,128]{1,0:T(8,128)(2,1)S(1)} %copy-done.6, bf16[8,264,128]{2,1,0:T(8,128)(2,1)S(1)} %all-to-all-done.1.cache_ref, ...), custom_call_target="tpu_custom_call" | custom-call | flops 805306368 | bytes 917504 | tf_op jit(solution)/shard_map/attend/pallas_call | solution.py:292
  65.1 25.4 %all_to_all.15.got_ref = bf16[8,192,128]{2,1,0:T(8,128)(2,1)S(1)} all-to-all(bf16[8,192,128]{2,1,0:T(8,128)(2,1)S(1)} %attend.1), channel_id=1, replica_groups=mesh['fsdp'=4,'tok'=8] {'tok'}, dimensions={0} | all-to-all | bytes 786432 | tf_op jit(solution)/shard_map/all_to_all | solution.py:307
  90.5 0.9 all-gather.2.cloned.1.call-done.w_ref
  91.4 1.6 %copy-done.1 = bf16[1024,1024]{1,0:T(8,128)(2,1)S(1)} copy-done((bf16[1024,1024]{1,0:T(8,128)(2,1)S(1)}, bf16[1024,1024]{1,0:T(8,128)(2,1)}, u32[]{:S(2)}) %copy-start.1) | copy-done | bytes 2097176
  93.0 1.1 %finish.1 = (bf16[64,1024]{1,0:T(8,128)(2,1)}, bf16[64,1024]{1,0:T(8,128)(2,1)}, bf16[64,1024]{1,0:T(8,128)(2,1)}) custom-call(bf16[8,192,128]{2,1,0:T(8,128)(2,1)S(1)} %all_to_all.15.got_ref, bf16[1024,1024]{1,0:T(8,128)(2,1)S(1)} %copy-done.1, bf16[64,1024]{1,0:T(8,128)(2,1)S(1)} %bitcast.38), custom_call_target="tpu_custom_call" | custom-call | flops 134217728 | bytes 2752512 | tf_op jit(solution)/shard_map/finish/pallas_call | solution.py:308
  (53 shorter events, 1.0 us)
Async XLA Ops:
  7.2 20.4 %copy-start = (f32[32,16]{0,1:T(8,128)S(1)}, f32[32,16]{0,1:T(8,128)}, u32[]{:S(2)}) copy-start(f32[32,16]{0,1:T(8,128)} %param.22) | copy-start | bytes 6148
  7.2 13.2 %copy-start.9 = (bf16[32,1024]{1,0:T(8,128)(2,1)S(1)}, bf16[32,1024]{1,0:T(8,128)(2,1)}, u32[]{:S(2)}) copy-start(bf16[32,1024]{1,0:T(8,128)(2,1)} %param.24) | copy-start | bytes 196612
  10.0 22.5 %collective-permute-start = (bf16[64,1024]{1,0:T(8,128)(2,1)}, bf16[64,1024]{1,0:T(8,128)(2,1)}, u32[]{:S(2)}, u32[]{:S(2)}) collective-permute-start(bf16[64,1024]{1,0:T(8,128)(2,1)} %get-tuple-element.44), channel_id=1, source_target_pairs={{0,2},{1,3},{2,4},{3,5},{4,6},{5,7},{6,0},{7,1},{8,10},{9,11},{10,... | collective-permute-start | bytes 393224 | tf_op jit(solution)/shard_map/ppermute | solution.py:233
  13.0 22.4 %collective-permute-start.1 = (bf16[64,1024]{1,0:T(8,128)(2,1)}, bf16[64,1024]{1,0:T(8,128)(2,1)}, u32[]{:S(2)}, u32[]{:S(2)}) collective-permute-start(bf16[64,1024]{1,0:T(8,128)(2,1)} %get-tuple-element.44), channel_id=1, source_target_pairs={{0,4},{1,5},{2,6},{3,7},{4,0},{5,1},{6,2},{7,3},{8,12},{9,13},{10,... | collective-permute-start | bytes 393224 | tf_op jit(solution)/shard_map/ppermute | solution.py:233
  15.6 26.8 %collective-permute-start.2 = (bf16[64,1024]{1,0:T(8,128)(2,1)}, bf16[64,1024]{1,0:T(8,128)(2,1)S(1)}, u32[]{:S(2)}, u32[]{:S(2)}) collective-permute-start(bf16[64,1024]{1,0:T(8,128)(2,1)} %get-tuple-element.44), channel_id=1, source_target_pairs={{0,6},{1,7},{2,0},{3,1},{4,2},{5,3},{6,4},{7,5},{8,14},{9,15},{10,... | collective-permute-start | bytes 393224 | tf_op jit(solution)/shard_map/ppermute | solution.py:233
  16.9 27.6 %collective-permute-start.3 = (bf16[64,1024]{1,0:T(8,128)(2,1)}, bf16[64,1024]{1,0:T(8,128)(2,1)}, u32[]{:S(2)}, u32[]{:S(2)}) collective-permute-start(bf16[64,1024]{1,0:T(8,128)(2,1)} %get-tuple-element.44), channel_id=1, source_target_pairs={{0,1},{1,0},{2,3},{3,2},{4,5},{5,4},{6,7},{7,6},{8,9},{9,8},{10,11... | collective-permute-start | bytes 393224 | tf_op jit(solution)/shard_map/ppermute | solution.py:238
  20.3 5.8 %copy-start.11 = (s32[1,64]{1,0:T(1,128)S(1)}, s32[1,64]{1,0:T(1,128)}, u32[]{:S(2)}) copy-start(s32[1,64]{1,0:T(1,128)} %param.20) | copy-start | bytes 772
  20.3 5.8 %copy-start.10 = (s32[1536]{0:T(1024)S(1)}, s32[1536]{0:T(1024)}, u32[]{:S(2)}) copy-start(s32[1536]{0:T(1024)} %param.21) | copy-start | bytes 18436
  20.3 5.9 %copy-start.7 = (bf16[1,128,1024]{2,1,0:T(8,128)(2,1)S(1)}, bf16[1,128,1024]{2,1,0:T(8,128)(2,1)}, u32[]{:S(2)}) copy-start(bf16[1,128,1024]{2,1,0:T(8,128)(2,1)} %param.18) | copy-start | bytes 786436
  21.0 5.6 %copy-start.8 = (bf16[1,128,1024]{2,1,0:T(8,128)(2,1)S(1)}, bf16[1,128,1024]{2,1,0:T(8,128)(2,1)}, u32[]{:S(2)}) copy-start(bf16[1,128,1024]{2,1,0:T(8,128)(2,1)} %param.17) | copy-start | bytes 786436
  21.9 13.7 %all-to-all-start = ((bf16[8,32,384]{2,1,0:T(8,128)(2,1)}), bf16[8,32,384]{2,1,0:T(8,128)(2,1)S(1)}, u32[]{:S(2)}, u32[]{:S(2)}) async-start(bf16[8,32,384]{2,1,0:T(8,128)(2,1)} %reshape.183), calls=%async_computation | async-start | bytes 393216 | tf_op jit(solution)/shard_map/all_to_all | solution.py:223
  25.3 66.2 %all-gather.2.cloned.1.call-start = ((), (), s32[]{:S(2)}) async-start(), calls=%async_computation.3 | async-start | bytes 2162688 | tf_op jit(solution)/shard_map/all_gather | solution.py:219
  26.0 1.1 %slice-start = ((s32[1536]{0:T(1024)}), s32[385]{0:T(512)S(1)}, s32[]{:S(2)}) async-start(s32[1536]{0:T(1024)} %param.21), calls=%async_computation.4 | async-start | bytes 4096 | tf_op jit(solution)/shard_map/slice | solution.py:26
  31.3 1.0 copy-start.3
  32.4 13.0 %collective-permute-start.4 = (bf16[64,1024]{1,0:T(8,128)(2,1)}, bf16[64,1024]{1,0:T(8,128)(2,1)}, u32[]{:S(2)}, u32[]{:S(2)}) collective-permute-start(bf16[64,1024]{1,0:T(8,128)(2,1)} %collective-permute-done), channel_id=1, source_target_pairs={{0,1},{1,0},{2,3},{3,2},{4,5},{5,4},{6,7},{7,6},{8,9},{9,8},{10,11... | collective-permute-start | bytes 393224 | tf_op jit(solution)/shard_map/ppermute | solution.py:238
  35.3 11.0 %collective-permute-start.5 = (bf16[64,1024]{1,0:T(8,128)(2,1)}, bf16[64,1024]{1,0:T(8,128)(2,1)}, u32[]{:S(2)}, u32[]{:S(2)}) collective-permute-start(bf16[64,1024]{1,0:T(8,128)(2,1)} %collective-permute-done.1), channel_id=1, source_target_pairs={{0,1},{1,0},{2,3},{3,2},{4,5},{5,4},{6,7},{7,6},{8,9},{9,8},{10,11... | collective-permute-start | bytes 393224 | tf_op jit(solution)/shard_map/ppermute | solution.py:238
  35.5 23.4 %all-to-all-start.1 = ((bf16[8,264,128]{2,1,0:T(8,128)(2,1)}), bf16[8,264,128]{2,1,0:T(8,128)(2,1)S(1)}, u32[]{:S(2)}, u32[]{:S(2)}) async-start(bf16[8,264,128]{2,1,0:T(8,128)(2,1)} %pad_maximum_fusion), calls=%async_computation.1 | async-start | bytes 1081344 | tf_op jit(solution)/shard_map/all_to_all | solution.py:259
  42.4 5.8 %collective-permute-start.6 = (bf16[64,1024]{1,0:T(8,128)(2,1)S(1)}, bf16[64,1024]{1,0:T(8,128)(2,1)S(1)}, u32[]{:S(2)}, u32[]{:S(2)}) collective-permute-start(bf16[64,1024]{1,0:T(8,128)(2,1)S(1)} %collective-permute-done.2), channel_id=1, source_target_pairs={{0,1},{1,0},{2,3},{3,2},{4,5},{5,4},{6,7},{7,6},{8,9},{9,8},{10,11... | collective-permute-start | bytes 393224 | tf_op jit(solution)/shard_map/ppermute | solution.py:238
  58.3 0.7 copy-start.5
  59.1 1.2 %copy-start.4 = (f32[2,128,1024]{2,1,0:T(8,128)S(1)}, f32[2,128,1024]{2,1,0:T(8,128)}, u32[]{:S(2)}) copy-start(f32[2,128,1024]{2,1,0:T(8,128)} %copy-done.3) | copy-start | bytes 3145732
  60.3 0.9 copy-start.6
  61.2 30.2 %copy-start.2 = (bf16[1,64,1024]{2,1,0:T(8,128)(2,1)S(1)}, bf16[1,64,1024]{2,1,0:T(8,128)(2,1)}, u32[]{:S(2)}) copy-start(bf16[1,64,1024]{2,1,0:T(8,128)(2,1)} %param.16) | copy-start | bytes 393220
  91.4 1.6 %copy-start.1 = (bf16[1024,1024]{1,0:T(8,128)(2,1)S(1)}, bf16[1024,1024]{1,0:T(8,128)(2,1)}, u32[]{:S(2)}) copy-start(bf16[1024,1024]{1,0:T(8,128)(2,1)} %all-gather.2.cloned.1.call-done.w_ref) | copy-start | bytes 6291460
Sparse Core Ops, SparseCore 0:
  29.1 62.3 all-gather.1

commit v2 on v1

v2 whole, which is shorter than its diff:
```python
import functools

import jax
import jax.numpy as jnp
from jax import lax
from jax.experimental import pallas as pl
from jax.experimental.pallas import tpu as pltpu
from jax.sharding import PartitionSpec as P

masked = -1e30
q_rows = 128
lanes = 128
slot_base = 32
mebibyte = 1024 * 1024
vmem_grants = {"attend": 60 * mebibyte}
vmem_grant = 16 * mebibyte


def fetch(pairs, sems):
    copies = [
        pltpu.make_async_copy(source, target, sems.at[at])
        for at, (source, target) in enumerate(pairs)
    ]
    for copy in copies:
        copy.start()
    return copies


def token_places(near):
    peers, me = lax.axis_size("tok"), lax.axis_index("tok")
    far_of = [lax.rem(me + peers - near * step, peers) for step in range(peers // near)]
    places = list(far_of)
    for turn in range(1, near):
        places += [
            one - lax.rem(one, near) + lax.rem(one + near - turn, near) for one in far_of
        ]
    return places


def fsdp_origins():
    count, me = lax.axis_size("fsdp"), lax.axis_index("fsdp")
    origins = [lax.rem(me + count - 2 * step, count) for step in range(count // 2)]
    return origins + [origin + 1 - 2 * lax.rem(origin, 2) for origin in origins]


def place_kernel(near, part_ref, out_ref, sems):
    places = token_places(near)
    rows, span = out_ref.shape[0] // len(places), part_ref.shape[0] // len(places)
    pairs = [
        (
            part_ref.at[pl.ds((at + 1) * span - rows, rows)],
            out_ref.at[pl.ds(pl.multiple_of(place * rows, rows), rows)],
        )
        for at, place in enumerate(places)
    ]
    for copy in fetch(pairs, sems):
        copy.wait()


def table_kernel(len_ref, bias_ref, bucket_ref, cache_out, new_out, cache_tab, new_tab, sems):
    heads, unused, reach = cache_tab.shape
    first_head = lax.axis_index("tok") * heads
    span = new_tab.shape[2]
    new_count = span // 2
    tiles = bucket_ref.shape[0]
    swap = lax.broadcasted_iota(jnp.int32, (lanes, lanes), 0) + lax.broadcasted_iota(
        jnp.int32, (lanes, lanes), 1
    )
    swap = (swap == lanes - 1).astype(jnp.bfloat16)
    buckets = bucket_ref[...].astype(jnp.float32).astype(jnp.bfloat16)
    turned = jnp.dot(buckets, swap, preferred_element_type=jnp.float32).astype(jnp.int32)
    row = jnp.concatenate([turned[at : at + 1, :] for at in reversed(range(tiles))], axis=1)
    row = jnp.broadcast_to(row, (8, reach))
    copies = []
    for h in range(heads):
        found = jnp.zeros((8, reach), jnp.float32)
        for bucket in range(bias_ref.shape[0]):
            found = jnp.where(row == bucket, bias_ref[bucket, first_head + h], found)
        after = jnp.full((8, new_count), masked, jnp.float32)
        bases = (
            pltpu.roll(found, len_ref[0] + (new_count - q_rows + 1), 1),
            pltpu.roll(jnp.concatenate([found[:, reach - new_count :], after], axis=1), span - q_rows + 1, 1),
        )
        for at, (base, tab, out) in enumerate(
            zip(bases, (cache_tab, new_tab), (cache_out, new_out))
        ):
            sublane = lax.broadcasted_iota(jnp.int32, base.shape, 0)
            for bit in (1, 2, 4):
                base = jnp.where((sublane & bit) != 0, pltpu.roll(base, bit, 1), base)
            for group in range(q_rows // 8):
                tab[h, group * 8 : (group + 1) * 8, :] = (
                    pltpu.roll(base, group * 8, 1) if group else base
                )
            copy = pltpu.make_async_copy(tab.at[h], out.at[h], sems.at[2 * h + at])
            copy.start()
            copies.append(copy)
    for copy in copies:
        copy.wait()


def attend_kernel(
    near,
    width,
    head_size,
    token_parts,
    weight_parts,
    len_ref,
    *refs,
):
    x_refs = refs[:token_parts]
    w_refs = refs[token_parts : token_parts + weight_parts]
    (
        cache_any,
        cache_tab_any,
        new_tab_any,
        out_ref,
        all_x,
        all_w,
        cache_ref,
        cache_tab,
        new_tab,
        q_ref,
        k_ref,
        v_ref,
        key_aug,
        val_aug,
        new_val_aug,
        sems,
    ) = refs[token_parts + weight_parts :]
    head_count = width // head_size
    peers = out_ref.shape[0]
    tok_rows = out_ref.shape[1] // 3
    new_count, full = q_ref.shape
    cache_rows = (cache_ref.shape[1] - 8) // 2
    cache_count = peers * cache_rows
    length = len_ref[0]
    pairs = [
        (
            x_refs[0].at[pl.ds(at * (x_refs[0].shape[0] // peers), tok_rows)],
            all_x.at[pl.ds(pl.multiple_of(place * tok_rows, tok_rows), tok_rows)],
        )
        for at, place in enumerate(token_places(near))
    ]
    pairs.append((w_refs[0], all_w))
    first = len(pairs)
    pairs += [(cache_any, cache_ref), (cache_tab_any, cache_tab), (new_tab_any, new_tab)]
    copies = fetch(pairs, sems)
    for copy in copies[:first]:
        copy.wait()
    made = jnp.dot(
        all_x[...],
        all_w[...],
        preferred_element_type=jnp.float32,
    ).astype(jnp.bfloat16)
    for part, ref in enumerate((q_ref, k_ref, v_ref)):
        piece = made[:, part * width : (part + 1) * width]
        if width < full:
            piece = jnp.concatenate(
                [piece, jnp.zeros((new_count, full - width), jnp.bfloat16)], axis=1
            )
        ref[...] = piece

    for copy in copies[first:]:
        copy.wait()
    told = cache_ref[:, 2 * cache_rows :, :].astype(jnp.float32)
    slots = jnp.concatenate(
        [
            told[peer, 0:1, :tok_rows] * slot_base + told[peer, 1:2, :tok_rows]
            for peer in range(peers)
        ],
        axis=1,
    ).astype(jnp.int32)
    slot_row = lax.broadcasted_iota(jnp.int32, (new_count, new_count), 0)
    deal = (slots == slot_row).astype(jnp.bfloat16)
    for part, ref in ((1, k_ref), (2, v_ref)):
        dealt = jnp.dot(deal, ref[...], preferred_element_type=jnp.float32).astype(jnp.bfloat16)
        for dest in range(peers):
            out_ref[dest, part * tok_rows : (part + 1) * tok_rows, :] = dealt[
                dest * tok_rows : (dest + 1) * tok_rows, :width
            ]

    old_keys = cache_ref[:, :cache_rows, :].reshape(cache_count, width)
    old_vals = cache_ref[:, cache_rows : 2 * cache_rows, :].reshape(cache_count, width)
    if width < full:
        blank = jnp.zeros((cache_count, full - width), jnp.bfloat16)
        old_keys = jnp.concatenate([old_keys, blank], axis=1)
        old_vals = jnp.concatenate([old_vals, blank], axis=1)
    key_row = lax.broadcasted_iota(jnp.int32, (cache_count, full), 0)
    key_lane = lax.broadcasted_iota(jnp.int32, (cache_count, full), 1)
    new_lane = lax.broadcasted_iota(jnp.int32, (new_count, full), 1)
    dead = jnp.where(key_row < length, 0.0, masked).astype(jnp.bfloat16)
    one = jnp.ones((), jnp.bfloat16)
    for h in range(head_count):
        spare = ((h + 1) * head_size) % full
        mine = (key_lane >= h * head_size) & (key_lane < (h + 1) * head_size)
        mine_new = (new_lane >= h * head_size) & (new_lane < (h + 1) * head_size)
        key_aug[h] = jnp.where(key_lane == spare, dead, old_keys)
        val_aug[h] = jnp.where(mine, old_vals, one)
        new_val_aug[h] = jnp.where(mine_new, v_ref[...], one)

    lane = lax.broadcasted_iota(jnp.int32, (q_rows, full), 1)
    per_dest = tok_rows
    for block in range(new_count // q_rows):
        q_here = q_ref[block * q_rows : (block + 1) * q_rows, :]
        start = new_count - q_rows - block * q_rows
        seen = (block + 1) * q_rows
        made = None
        for h in range(head_count):
            spare = ((h + 1) * head_size) % full
            mine = (lane >= h * head_size) & (lane < (h + 1) * head_size)
            q_new = jnp.where(mine, q_here, jnp.zeros((), jnp.bfloat16))
            q_old = jnp.where(lane == spare, one, q_new)
            s_old = lax.dot_general(
                q_old, key_aug[h], (((1,), (1,)), ((), ())), preferred_element_type=jnp.float32
            )
            s_new = lax.dot_general(
                q_new,
                k_ref[:seen, :],
                (((1,), (1,)), ((), ())),
                preferred_element_type=jnp.float32,
            )
            s_old = s_old + cache_tab[h, :, start : start + cache_count]
            s_new = s_new + new_tab[h, :, start : start + seen]
            peak = jnp.maximum(
                jnp.max(s_old, axis=1, keepdims=True), jnp.max(s_new, axis=1, keepdims=True)
            )
            p_old = jnp.exp(s_old - peak).astype(jnp.bfloat16)
            p_new = jnp.exp(s_new - peak).astype(jnp.bfloat16)
            total = jnp.dot(p_old, val_aug[h], preferred_element_type=jnp.float32) + jnp.dot(
                p_new, new_val_aug[h, :seen, :], preferred_element_type=jnp.float32
            )
            part = total / total[:, spare : spare + 1]
            made = part if made is None else jnp.where(mine, part, made)
        made = made.astype(jnp.bfloat16)
        for piece in range(q_rows // per_dest):
            out_ref[block * (q_rows // per_dest) + piece, :per_dest, :] = made[
                piece * per_dest : (piece + 1) * per_dest, :width
            ]


def finish_kernel(got_ref, states_ref, *refs):
    w_refs = refs[:-6]
    hidden_ref, keys_ref, values_ref, all_w, context, sems = refs[-6:]
    peers = got_ref.shape[0]
    rows, features = states_ref.shape
    depth = w_refs[0].shape[0]
    copies = fetch([(w_ref, all_w.at[part]) for part, w_ref in enumerate(w_refs)], sems)
    for part, ref in ((1, keys_ref), (2, values_ref)):
        ref[...] = jnp.concatenate(
            [got_ref[p, part * rows : (part + 1) * rows, :] for p in range(peers)], axis=1
        )
    context[...] = jnp.concatenate([got_ref[p, :rows, :] for p in range(peers)], axis=1)
    made = states_ref[...].astype(jnp.float32)
    for part, (copy, origin) in enumerate(zip(copies, fsdp_origins())):
        copy.wait()
        spot = pl.multiple_of(origin * depth, depth)
        made = made + jnp.dot(
            context[:, pl.ds(spot, depth)], all_w[part], preferred_element_type=jnp.float32
        )
    hidden_ref[...] = made.astype(jnp.bfloat16)


def vmem():
    return pl.BlockSpec(memory_space=pltpu.VMEM)


def hbm():
    return pl.BlockSpec(memory_space=pltpu.HBM)


def smem():
    return pl.BlockSpec(memory_space=pltpu.SMEM)


def call(kernel, outs, specs, scratch, name, flops, moved, kind=jnp.bfloat16, out_space=vmem):
    return pl.pallas_call(
        kernel,
        out_shape=[jax.ShapeDtypeStruct(shape, kind) for shape in outs],
        in_specs=specs,
        out_specs=[out_space() for unused in outs],
        scratch_shapes=scratch,
        name=name,
        cost_estimate=pl.CostEstimate(flops=flops, bytes_accessed=moved, transcendentals=0),
        compiler_params=pltpu.CompilerParams(vmem_limit_bytes=vmem_grants.get(name, vmem_grant)),
    )


def shards(
    near,
    states,
    cache_keys,
    cache_values,
    cache_len,
    token_slot,
    bucket_table,
    rel_bias,
    norm_gain,
    w_query,
    w_key,
    w_value,
    w_out,
):
    peers = lax.axis_size("tok")
    tokens = states[0]
    tok_rows, features = tokens.shape
    heads = rel_bias.shape[1]
    head_size = features // heads
    width = features // peers
    my_heads = width // head_size
    new_count = tok_rows * peers
    cache_rows = cache_keys.shape[1]

    fsdp_count = lax.axis_size("fsdp")
    far = peers // near

    def over_tok(parts, turns):
        return [lax.ppermute(part, "tok", turns) for part in parts]

    def far_turn(step):
        return [(t, (t + near * step) % peers) for t in range(peers)]

    def near_turn(step):
        return [(t, t - t % near + (t + step) % near) for t in range(peers)]

    def gather_fsdp(part):
        parts = [part]
        for step in range(1, fsdp_count // 2):
            turn = [(f, (f + 2 * step) % fsdp_count) for f in range(fsdp_count)]
            parts.append(lax.ppermute(part, "fsdp", turn))
        swap = [(f, f ^ 1) for f in range(fsdp_count)]
        return parts + [lax.ppermute(one, "fsdp", swap) for one in parts]

    sent_w = jnp.stack([w_query, w_key, w_value], axis=1).reshape(-1, 3, peers, width)
    sent_w = jnp.transpose(sent_w, (2, 0, 1, 3)).reshape(peers, -1, 3 * width)
    got_w = lax.all_to_all(sent_w, "tok", split_axis=0, concat_axis=0, tiled=True)

    reach = bucket_table.shape[0]
    shapes = [(my_heads, q_rows, reach), (my_heads, q_rows, 2 * new_count)]
    cache_tab, new_tab = call(
        table_kernel,
        shapes,
        [smem()] * 2 + [vmem()],
        [pltpu.VMEM(shape, jnp.float32) for shape in shapes]
        + [pltpu.SemaphoreType.DMA((2 * my_heads,))],
        "tables",
        0,
        4 * my_heads * q_rows * (reach + 2 * new_count),
        jnp.float32,
        hbm,
    )(
        cache_len,
        rel_bias,
        bucket_table.reshape(reach // lanes, lanes),
    )

    got_w, cache_tab, new_tab = lax.optimization_barrier((got_w, cache_tab, new_tab))
    my_w = [lax.all_gather(got_w.reshape(-1, 3 * width), "fsdp", axis=0, tiled=True)]

    wide_in = tokens.astype(jnp.float32)
    inverse = lax.rsqrt(jnp.mean(wide_in * wide_in, axis=-1, keepdims=True) + 1e-06)
    normed = (wide_in * inverse * norm_gain).astype(jnp.bfloat16)
    out_rows = w_out.shape[0]
    normed = jnp.concatenate([normed, w_out])
    parts = [normed] + [lax.ppermute(normed, "tok", far_turn(step)) for step in range(1, far)]
    for turn in range(1, near):
        parts += over_tok(parts[:far], near_turn(turn))

    *parts, weights = lax.optimization_barrier((*parts, my_w[0]))
    my_w = [weights]
    parts = [jnp.concatenate(parts)]

    def columns(rows):
        return jnp.transpose(rows.reshape(-1, peers, width), (1, 0, 2))

    slots = token_slot[0]
    note = jnp.zeros((8, width), jnp.bfloat16)
    note = note.at[0, :tok_rows].set((slots // slot_base).astype(jnp.bfloat16))
    note = note.at[1, :tok_rows].set((slots % slot_base).astype(jnp.bfloat16))
    sent_cache = jnp.concatenate(
        [
            columns(cache_keys[0]),
            columns(cache_values[0]),
            jnp.broadcast_to(note[None], (peers, 8, width)),
        ],
        axis=1,
    )
    cache = lax.all_to_all(sent_cache, "tok", split_axis=0, concat_axis=0, tiled=True)

    (out_tok,) = call(
        functools.partial(place_kernel, near),
        [(peers * out_rows, features)],
        [hbm()],
        [pltpu.SemaphoreType.DMA((peers,))],
        "place",
        0,
        4 * peers * out_rows * features,
    )(*parts)
    out_w = gather_fsdp(out_tok)

    full = max(width, lanes)
    cache_count = peers * cache_rows
    (sent,) = call(
        functools.partial(attend_kernel, near, width, head_size, len(parts), len(my_w)),
        [(peers, 3 * tok_rows, width)],
        [smem()] + [hbm()] * (len(parts) + len(my_w) + 3),
        [
            pltpu.VMEM((new_count, features), jnp.bfloat16),
            pltpu.VMEM((features, 3 * width), jnp.bfloat16),
            pltpu.VMEM(cache.shape, jnp.bfloat16),
            pltpu.VMEM(cache_tab.shape, jnp.float32),
            pltpu.VMEM(new_tab.shape, jnp.float32),
        ]
        + [pltpu.VMEM((new_count, full), jnp.bfloat16)] * 3
        + [
            pltpu.VMEM((my_heads, cache_count, full), jnp.bfloat16),
            pltpu.VMEM((my_heads, cache_count, full), jnp.bfloat16),
            pltpu.VMEM((my_heads, new_count, full), jnp.bfloat16),
            pltpu.SemaphoreType.DMA((peers + len(my_w) + 3,)),
        ],
        "attend",
        6 * new_count * features * width
        + 4 * my_heads * new_count * (new_count + cache_count) * full,
        2 * features * (new_count + 3 * width) + 4 * full * cache_count,
    )(cache_len, *parts, *my_w, cache, cache_tab, new_tab)

    got = lax.all_to_all(sent, "tok", split_axis=0, concat_axis=0, tiled=True)
    hidden, new_keys, new_values = call(
        finish_kernel,
        [(tok_rows, features)] * 3,
        [vmem()] * 2 + [hbm()] * len(out_w),
        [
            pltpu.VMEM((fsdp_count,) + out_tok.shape, jnp.bfloat16),
            pltpu.VMEM((tok_rows, features), jnp.bfloat16),
            pltpu.SemaphoreType.DMA((len(out_w),)),
        ],
        "finish",
        2 * tok_rows * features * features,
        2 * features * (features + 5 * tok_rows),
    )(got, tokens, *out_w)
    return (hidden[None], new_keys[None], new_values[None])


def solution(mesh):
    in_specs = (
        P("fsdp", "tok", None),
        P("fsdp", "tok", None),
        P("fsdp", "tok", None),
        P("fsdp"),
        P("fsdp", "tok"),
        P(),
        P(),
        P(),
        P(("fsdp", "tok"), None),
        P(("fsdp", "tok"), None),
        P(("fsdp", "tok"), None),
        P(("fsdp", "tok"), None),
    )
    out_specs = (P("fsdp", "tok", None), P("fsdp", "tok", None), P("fsdp", "tok", None))
    near = 2 if mesh.shape["tok"] <= 8 else 4
    return jax.shard_map(
        functools.partial(shards, near),
        mesh=mesh,
        in_specs=in_specs,
        out_specs=out_specs,
        check_vma=False,
    )
```

time: 102 us -> 78.2 us (0.77)
  blocking collectives: 34 us -> 9.03 us
  between operations: 15.2 us -> 1.6 us
  waiting for transfers between devices: 2.57 us -> 10.6 us
  starting transfers between devices: 22.1 us -> 28.4 us
  Pallas kernels: 8.07 us -> 12.8 us
  local copies, waits for them, and re-layouts: 14.5 us -> 10.9 us
    all_to_all x1 -> x0, blocking collectives: 25.4 us -> none  [shards(): got = lax.all_to_all(sent, 'tok', split_axis=0, concat_axis=0, tiled=True)]
    all_to_all x0 -> x1, waiting for transfers between devices: none -> 8.45 us  [shards(): got = lax.all_to_all(sent, 'tok', split_axis=0, concat_axis=0, tiled=True)]
    all_to_all x0 -> x1, starting transfers between devices: none -> 5.86 us  [shards(): got = lax.all_to_all(sent, 'tok', split_axis=0, concat_axis=0, tiled=True)]
    pallas_call x4, Pallas kernels: 8.07 us -> 12.8 us  [the longest x1 7.23 us: shards(): call(functools.partial(attend_kernel, near, width, head_size, len(parts),...]
    unnamed x39 -> x41, local copies, waits for them, and re-layouts: 12.4 us -> 8.33 us
    ppermute x7 -> x10, starting transfers between devices: 12.7 us -> 14.5 us  [the longest x3 7.01 us: shards(): lax.ppermute(normed, 'tok', far_turn(step))]
    unnamed x1 -> x0, other arithmetic: 1.68 us -> none
    all_to_all x1, starting transfers between devices: 5.92 us -> 4.58 us  [shards(): lax.all_to_all(sent_cache, 'tok', split_axis=0, concat_axis=0, tiled=True)]
  transfers between devices with their start and end apart: 10 -> 13, of which waited for: 2 -> 3; matrix products, arithmetic and copies ran while one was open for 11% -> 9% of each run, Pallas kernels for 7% -> 15%
where the time goes in v2:
time: 78.2 us; the launch traced here: 77.6 us
  starting transfers between devices  28.4 us (36%)
  Pallas kernels  12.8 us (16%)
  local copies, waits for them, and re-layouts  10.9 us (14%)
  waiting for transfers between devices  10.6 us (14%)
  blocking collectives  9.03 us (12%)
  other arithmetic  4.3 us (5%)
  between operations  1.6 us (2%)
    all_gather x1, blocking collectives, shards(): lax.all_gather(got_w.reshape(-1, 3 * width), 'fsdp', axis=0, tiled=True)  9.03 us
    all_to_all x1, waiting for transfers between devices, shards(): got = lax.all_to_all(sent, 'tok', split_axis=0, concat_axis=0, tiled=True)  8.45 us
    unnamed x41, local copies, waits for them, and re-layouts  8.33 us
    pallas_call x1, Pallas kernels, shards(): call(functools.partial(attend_kernel, near, width, head_size, len(parts),...  7.23 us
    ppermute x3, starting transfers between devices, shards(): lax.ppermute(normed, 'tok', far_turn(step))  7.01 us
    all_to_all x1, starting transfers between devices, shards(): got = lax.all_to_all(sent, 'tok', split_axis=0, concat_axis=0, tiled=True)  5.86 us
    ppermute x4, starting transfers between devices, over_tok(): return [lax.ppermute(part, 'tok', turns) for part in parts]  5.46 us
    all_to_all x1, starting transfers between devices, shards(): lax.all_to_all(sent_cache, 'tok', split_axis=0, concat_axis=0, tiled=True)  4.58 us
  transfers between devices with their start and end apart: 13, of which 3 were waited for; matrix products, arithmetic and copies ran while one was open for 9% of the time, Pallas kernels for 15%

profile of v2, /device:TPU:0, one launch (start us, length us, event | category | flops | bytes accessed | tf_op | source)
XLA Modules:
  0.0 77.6 jit_solution(12556177584052244268)
XLA Ops:
  0.6 1.0 %fusion = f32[64]{0:T(128)S(1)} fusion(bf16[1,64,1024]{2,1,0:T(8,128)(2,1)} %param.16), kind=kLoop, calls=%fused_computation.3 | loop fusion | flops 196544 | bytes 131328 | tf_op jit(solution)/shard_map/reduce_sum | solution.py:360
  1.7 0.0 copy-start.13
  1.7 1.1 %fusion.2 = bf16[64,1024]{1,0:T(8,128)(2,1)S(1)} fusion(f32[1024]{0:T(1024)} %param.23, f32[64]{0:T(128)S(1)} %add_rsqrt_fusion, bf16[1,64,1024]{2,1,0:T(8,128)(2,1)} %param.16), kind=kLoop, calls=%fused_computation.5 | loop fusion | flops 262144 | bytes 266496 | tf_op jit(solution)/shard_map/convert_element_type | solution.py:361
  2.8 0.9 %pad_maximum_fusion.1 = bf16[96,1024]{1,0:T(8,128)(2,1)S(1)} fusion(bf16[32,1024]{1,0:T(8,128)(2,1)} %param.27, bf16[64,1024]{1,0:T(8,128)(2,1)S(1)} %fusion.2), kind=kLoop, calls=%fused_computation.7 | loop fusion | flops 393216 | bytes 393216 | tf_op jit(solution)/shard_map/concatenate | solution.py:363
  3.6 3.1 %collective-permute-start = (bf16[96,1024]{1,0:T(8,128)(2,1)S(1)}, bf16[96,1024]{1,0:T(8,128)(2,1)S(1)}, u32[]{:S(2)}, u32[]{:S(2)}) collective-permute-start(bf16[96,1024]{1,0:T(8,128)(2,1)S(1)} %pad_maximum_fusion.1), channel_id=1, source_target_pairs={{0,2},{1,3},{2,4},{3,5},{4,6},{5,7},{6,0},{7,1},{8,10},{9,11},{10,... | collective-permute-start | bytes 589832 | tf_op jit(solution)/shard_map/ppermute | solution.py:364
  6.7 2.6 %collective-permute-start.1 = (bf16[96,1024]{1,0:T(8,128)(2,1)S(1)}, bf16[96,1024]{1,0:T(8,128)(2,1)S(1)}, u32[]{:S(2)}, u32[]{:S(2)}) collective-permute-start(bf16[96,1024]{1,0:T(8,128)(2,1)S(1)} %pad_maximum_fusion.1), channel_id=1, source_target_pairs={{0,4},{1,5},{2,6},{3,7},{4,0},{5,1},{6,2},{7,3},{8,12},{9,13},{10,... | collective-permute-start | bytes 589832 | tf_op jit(solution)/shard_map/ppermute | solution.py:364
  9.3 1.3 %collective-permute-start.2 = (bf16[96,1024]{1,0:T(8,128)(2,1)S(1)}, bf16[96,1024]{1,0:T(8,128)(2,1)S(1)}, u32[]{:S(2)}, u32[]{:S(2)}) collective-permute-start(bf16[96,1024]{1,0:T(8,128)(2,1)S(1)} %pad_maximum_fusion.1), channel_id=1, source_target_pairs={{0,6},{1,7},{2,0},{3,1},{4,2},{5,3},{6,4},{7,5},{8,14},{9,15},{10,... | collective-permute-start | bytes 589832 | tf_op jit(solution)/shard_map/ppermute | solution.py:364
  10.7 1.5 %collective-permute-start.3 = (bf16[96,1024]{1,0:T(8,128)(2,1)S(1)}, bf16[96,1024]{1,0:T(8,128)(2,1)S(1)}, u32[]{:S(2)}, u32[]{:S(2)}) collective-permute-start(bf16[96,1024]{1,0:T(8,128)(2,1)S(1)} %pad_maximum_fusion.1), channel_id=1, source_target_pairs={{0,1},{1,0},{2,3},{3,2},{4,5},{5,4},{6,7},{7,6},{8,9},{9,8},{10,11... | collective-permute-start | bytes 589832 | tf_op jit(solution)/shard_map/ppermute | solution.py:317
  12.2 0.8 %copy.25 = bf16[4,8,8,128]{3,2,1,0:T(8,128)(2,1)S(1)} copy(bf16[4,8,8,128]{3,1,2,0:T(8,128)(2,1)} %bitcast.36) | data formatting | bytes 131072
  13.0 0.1 copy.17
  13.1 0.9 %copy.26 = bf16[4,8,8,128]{3,2,1,0:T(8,128)(2,1)S(1)} copy(bf16[4,8,8,128]{3,1,2,0:T(8,128)(2,1)} %bitcast.37) | data formatting | bytes 131072
  14.0 0.1 copy.18
  14.1 0.9 %copy.27 = bf16[4,8,8,128]{3,2,1,0:T(8,128)(2,1)S(1)} copy(bf16[4,8,8,128]{3,1,2,0:T(8,128)(2,1)} %bitcast.38) | data formatting | bytes 131072
  15.0 0.1 copy.19
  15.1 0.5 maximum_bitcast_fusion
  15.6 0.9 %reshape.92 = bf16[8,32,384]{2,1,0:T(8,128)(2,1)} reshape(bf16[8,32,3,128]{3,2,1,0:T(4,128)(2,1)S(1)} %maximum_bitcast_fusion) | data formatting | bytes 393216 | tf_op jit(solution)/shard_map/reshape | solution.py:334
  16.4 3.4 %all-to-all-start = ((bf16[8,32,384]{2,1,0:T(8,128)(2,1)}), bf16[8,32,384]{2,1,0:T(8,128)(2,1)S(1)}, u32[]{:S(2)}, u32[]{:S(2)}) async-start(bf16[8,32,384]{2,1,0:T(8,128)(2,1)} %reshape.92), calls=%async_computation | async-start | bytes 393216 | tf_op jit(solution)/shard_map/all_to_all | solution.py:335
  20.5 0.1 copy.20.bias_ref
  20.6 0.2 copy.21
  20.7 0.2 copy.22
  21.0 0.2 copy.23
  21.1 0.2 copy.24
  21.3 3.3 %tables.1 = (f32[2,128,1536]{2,1,0:T(8,128)S(1)}, f32[2,128,1024]{2,1,0:T(8,128)S(1)}) custom-call(s32[1]{0:T(128)S(6)} %copy.36.len_ref, f32[32,16]{1,0:T(8,128)S(1)} %copy.20.bias_ref, s32[12,128]{1,0:T(8,128)S(1)} %bitcast.27), custom_call_target="tpu_custom_call" | custom-call | bytes 2621440 | tf_op jit(solution)/shard_map/tables/pallas_call | solution.py:339
  24.7 1.2 %copy-done.1 = f32[2,128,1536]{2,1,0:T(8,128)} copy-done((f32[2,128,1536]{2,1,0:T(8,128)}, f32[2,128,1536]{2,1,0:T(8,128)S(1)}, u32[]{:S(2)}) %copy-start.1) | copy-done | bytes 1572888
  25.9 1.0 %copy-done.3 = f32[2,128,1024]{2,1,0:T(8,128)} copy-done((f32[2,128,1024]{2,1,0:T(8,128)}, f32[2,128,1024]{2,1,0:T(8,128)S(1)}, u32[]{:S(2)}) %copy-start.3) | copy-done | bytes 1048600
  26.8 0.1 scatter.9
  26.9 0.9 %pad_maximum_fusion = bf16[8,264,128]{2,1,0:T(8,128)(2,1)} fusion(bf16[8,8,128]{2,1,0:T(8,128)(2,1)S(1)} %broadcast_in_dim.8, bf16[8,128,128]{2,1,0:T(8,128)(2,1)S(1)} %bitcast.31, bf16[8,128,128]{2,1,0:T(8,128)(2,1)S(1)} %bitcast.30), kind=kLoop, calls=%fused_computation | loop fusion | flops 1622016 | bytes 1081344 | tf_op jit(solution)/shard_map/concatenate | solution.py:379
  27.8 1.9 %collective-permute-start.4 = (bf16[96,1024]{1,0:T(8,128)(2,1)S(1)}, bf16[96,1024]{1,0:T(8,128)(2,1)S(1)}, u32[]{:S(2)}, u32[]{:S(2)}) collective-permute-start(bf16[96,1024]{1,0:T(8,128)(2,1)S(1)} %collective-permute-done), channel_id=1, source_target_pairs={{0,1},{1,0},{2,3},{3,2},{4,5},{5,4},{6,7},{7,6},{8,9},{9,8},{10,11... | collective-permute-start | bytes 589832 | tf_op jit(solution)/shard_map/ppermute | solution.py:317
  29.7 0.1 collective-permute-start.5
  29.8 1.9 %collective-permute-start.6 = (bf16[96,1024]{1,0:T(8,128)(2,1)S(1)}, bf16[96,1024]{1,0:T(8,128)(2,1)}, u32[]{:S(2)}, u32[]{:S(2)}) collective-permute-start(bf16[96,1024]{1,0:T(8,128)(2,1)S(1)} %collective-permute-done.2), channel_id=1, source_target_pairs={{0,1},{1,0},{2,3},{3,2},{4,5},{5,4},{6,7},{7,6},{8,9},{9,8},{10,11... | collective-permute-start | bytes 589832 | tf_op jit(solution)/shard_map/ppermute | solution.py:317
  31.7 4.6 %all-to-all-start.1 = ((bf16[8,264,128]{2,1,0:T(8,128)(2,1)}), bf16[8,264,128]{2,1,0:T(8,128)(2,1)S(1)}, u32[]{:S(2)}, u32[]{:S(2)}) async-start(bf16[8,264,128]{2,1,0:T(8,128)(2,1)} %pad_maximum_fusion), calls=%async_computation.1 | async-start | bytes 1081344 | tf_op jit(solution)/shard_map/all_to_all | solution.py:387
  36.3 9.0 %all_gather.3.refs_1_ = bf16[1024,384]{1,0:T(8,128)(2,1)} all-gather(bf16[256,384]{1,0:T(8,128)(2,1)S(1)} %bitcast.32), channel_id=1, replica_groups=mesh['fsdp'=4,'tok'=8] {'fsdp'}, dimensions={0}, use_global_device_ids=true | all-gather | bytes 983040 | tf_op jit(solution)/shard_map/all_gather | solution.py:357
  45.4 0.7 copy-done.8
  46.0 0.7 copy-done.10
  46.7 0.0 collective-permute-done.6
  46.8 0.8 %copy-done.9 = bf16[96,1024]{1,0:T(8,128)(2,1)S(1)} copy-done((bf16[96,1024]{1,0:T(8,128)(2,1)S(1)}, bf16[96,1024]{1,0:T(8,128)(2,1)}, u32[]{:S(2)}) %copy-start.9) | copy-done | bytes 196632
  47.7 0.1 copy-done.11
  47.8 0.9 %constant_dynamic-update-slice_fusion.refs_0_.part_ref = bf16[768,1024]{1,0:T(8,128)(2,1)S(1)} fusion(bf16[768,1024]{1,0:T(8,128)(2,1)S(1)} %constant_dynamic-update-slice_fusion.1, bf16[96,1024]{1,0:T(8,128)(2,1)} %collective-permute-done.6), kind=kLoop, calls=%fused_computation.8 | loop fusion | bytes 393216 | tf_op jit(solution)/shard_map/concatenate | solution.py:370
  48.7 0.8 %place.1.refs_0_ = bf16[256,1024]{1,0:T(8,128)(2,1)S(1)} custom-call(bf16[768,1024]{1,0:T(8,128)(2,1)S(1)} %constant_dynamic-update-slice_fusion.refs_0_.part_ref), custom_call_target="tpu_custom_call" | custom-call | bytes 1048576 | tf_op jit(solution)/shard_map/place/pallas_call | solution.py:389
  49.5 1.6 %collective-permute-start.7 = (bf16[256,1024]{1,0:T(8,128)(2,1)S(1)}, bf16[256,1024]{1,0:T(8,128)(2,1)S(1)}, u32[]{:S(2)}, u32[]{:S(2)}) collective-permute-start(bf16[256,1024]{1,0:T(8,128)(2,1)S(1)} %place.1.refs_0_), channel_id=1, source_target_pairs={{0,16},{8,24},{16,0},{24,8},{1,17},{9,25},{17,1},{25,9},{2,18},{10... | collective-permute-start | bytes 1572872 | tf_op jit(solution)/shard_map/ppermute | solution.py:329
  51.1 0.8 %copy-done.5 = bf16[8,264,128]{2,1,0:T(8,128)(2,1)} copy-done((bf16[8,264,128]{2,1,0:T(8,128)(2,1)}, bf16[8,264,128]{2,1,0:T(8,128)(2,1)S(1)}, u32[]{:S(2)}) %copy-start.5) | copy-done | bytes 540696
  51.9 7.2 %attend.1 = bf16[8,192,128]{2,1,0:T(8,128)(2,1)} custom-call(s32[1]{0:T(128)S(6)} %copy.36.len_ref, bf16[768,1024]{1,0:T(8,128)(2,1)} %copy-done, bf16[1024,384]{1,0:T(8,128)(2,1)} %all_gather.3.refs_1_, bf16[8,264,128]{2,1,0:T(8,128)(2,1)} %copy-done.5, f32[2,128,1536]{2,1,0:T(8,128)} %copy-done.1, f32[2,128,1024]{2,1,0:T(8,128)} %copy-done.3), custom_call_target="tpu_custom_call" | custom-call | flops 1207959552 | bytes 2359296 | tf_op jit(solution)/shard_map/attend/pallas_call | solution.py:402
  59.2 5.9 %all-to-all-start.2 = ((bf16[8,192,128]{2,1,0:T(8,128)(2,1)}), bf16[8,192,128]{2,1,0:T(8,128)(2,1)S(1)}, u32[]{:S(2)}, u32[]{:S(2)}) async-start(bf16[8,192,128]{2,1,0:T(8,128)(2,1)} %attend.1), calls=%async_computation.2 | async-start | bytes 786432 | tf_op jit(solution)/shard_map/all_to_all | solution.py:426
  65.0 0.5 collective-permute-start.9
  65.5 1.4 %collective-permute-done.8.refs_2_ = bf16[256,1024]{1,0:T(8,128)(2,1)S(1)} collective-permute-done((bf16[256,1024]{1,0:T(8,128)(2,1)S(1)}, bf16[256,1024]{1,0:T(8,128)(2,1)S(1)}, u32[]{:S(2)}, u32[]{:S(2)}) %collective-permute-start.8) | collective-permute-done | bytes 524320 | tf_op jit(solution)/shard_map/ppermute | solution.py:331
  66.9 0.7 collective-permute-done.9.refs_3_
  67.7 8.4 %all-to-all-done.2.got_ref = bf16[8,192,128]{2,1,0:T(8,128)(2,1)S(1)} async-done(((bf16[8,192,128]{2,1,0:T(8,128)(2,1)}), bf16[8,192,128]{2,1,0:T(8,128)(2,1)S(1)}, u32[]{:S(2)}, u32[]{:S(2)}) %all-to-all-start.2) | async-done | bytes 393248 | tf_op jit(solution)/shard_map/all_to_all | solution.py:426
  76.1 1.4 %finish.1 = (bf16[64,1024]{1,0:T(8,128)(2,1)}, bf16[64,1024]{1,0:T(8,128)(2,1)}, bf16[64,1024]{1,0:T(8,128)(2,1)}) custom-call(bf16[8,192,128]{2,1,0:T(8,128)(2,1)S(1)} %all-to-all-done.2.got_ref, bf16[64,1024]{1,0:T(8,128)(2,1)S(1)} %bitcast.26, bf16[256,1024]{1,0:T(8,128)(2,1)S(1)} %place.1.refs_0_, bf16[256,1024]{1,0:T(8,128)(2,1)S(1)} %collective-permute-done.7.refs_1_, ...), custom_call_target="tpu_custom_call" | custom-call | flops 134217728 | bytes 2752512 | tf_op jit(solution)/shard_map/finish/pallas_call | solution.py:427
  (41 shorter events, 0.2 us)
Async XLA Ops:
  1.7 18.1 %copy-start.13 = (s32[1,64]{1,0:T(1,128)S(1)}, s32[1,64]{1,0:T(1,128)}, u32[]{:S(2)}) copy-start(s32[1,64]{1,0:T(1,128)} %param.20) | copy-start | bytes 772
  1.7 18.8 %copy-start.12 = (f32[32,16]{0,1:T(8,128)S(1)}, f32[32,16]{0,1:T(8,128)}, u32[]{:S(2)}) copy-start(f32[32,16]{0,1:T(8,128)} %param.22) | copy-start | bytes 6148
  1.7 18.9 %copy-start.6 = (bf16[1,128,1024]{2,1,0:T(8,128)(2,1)S(1)}, bf16[1,128,1024]{2,1,0:T(8,128)(2,1)}, u32[]{:S(2)}) copy-start(bf16[1,128,1024]{2,1,0:T(8,128)(2,1)} %param.17) | copy-start | bytes 786436
  3.6 24.1 %collective-permute-start = (bf16[96,1024]{1,0:T(8,128)(2,1)S(1)}, bf16[96,1024]{1,0:T(8,128)(2,1)S(1)}, u32[]{:S(2)}, u32[]{:S(2)}) collective-permute-start(bf16[96,1024]{1,0:T(8,128)(2,1)S(1)} %pad_maximum_fusion.1), channel_id=1, source_target_pairs={{0,2},{1,3},{2,4},{3,5},{4,6},{5,7},{6,0},{7,1},{8,10},{9,11},{10,... | collective-permute-start | bytes 589832 | tf_op jit(solution)/shard_map/ppermute | solution.py:364
  6.7 23.0 %collective-permute-start.1 = (bf16[96,1024]{1,0:T(8,128)(2,1)S(1)}, bf16[96,1024]{1,0:T(8,128)(2,1)S(1)}, u32[]{:S(2)}, u32[]{:S(2)}) collective-permute-start(bf16[96,1024]{1,0:T(8,128)(2,1)S(1)} %pad_maximum_fusion.1), channel_id=1, source_target_pairs={{0,4},{1,5},{2,6},{3,7},{4,0},{5,1},{6,2},{7,3},{8,12},{9,13},{10,... | collective-permute-start | bytes 589832 | tf_op jit(solution)/shard_map/ppermute | solution.py:364
  9.3 20.5 %collective-permute-start.2 = (bf16[96,1024]{1,0:T(8,128)(2,1)S(1)}, bf16[96,1024]{1,0:T(8,128)(2,1)S(1)}, u32[]{:S(2)}, u32[]{:S(2)}) collective-permute-start(bf16[96,1024]{1,0:T(8,128)(2,1)S(1)} %pad_maximum_fusion.1), channel_id=1, source_target_pairs={{0,6},{1,7},{2,0},{3,1},{4,2},{5,3},{6,4},{7,5},{8,14},{9,15},{10,... | collective-permute-start | bytes 589832 | tf_op jit(solution)/shard_map/ppermute | solution.py:364
  10.7 34.7 %collective-permute-start.3 = (bf16[96,1024]{1,0:T(8,128)(2,1)S(1)}, bf16[96,1024]{1,0:T(8,128)(2,1)S(1)}, u32[]{:S(2)}, u32[]{:S(2)}) collective-permute-start(bf16[96,1024]{1,0:T(8,128)(2,1)S(1)} %pad_maximum_fusion.1), channel_id=1, source_target_pairs={{0,1},{1,0},{2,3},{3,2},{4,5},{5,4},{6,7},{7,6},{8,9},{9,8},{10,11... | collective-permute-start | bytes 589832 | tf_op jit(solution)/shard_map/ppermute | solution.py:317
  14.0 6.9 %copy-start.7 = (bf16[1,128,1024]{2,1,0:T(8,128)(2,1)S(1)}, bf16[1,128,1024]{2,1,0:T(8,128)(2,1)}, u32[]{:S(2)}) copy-start(bf16[1,128,1024]{2,1,0:T(8,128)(2,1)} %param.18) | copy-start | bytes 786436
  15.5 5.8 %copy-start.4 = (s32[1536]{0:T(1024)S(1)}, s32[1536]{0:T(1024)}, u32[]{:S(2)}) copy-start(s32[1536]{0:T(1024)} %param.21) | copy-start | bytes 18436
  16.4 15.3 %all-to-all-start = ((bf16[8,32,384]{2,1,0:T(8,128)(2,1)}), bf16[8,32,384]{2,1,0:T(8,128)(2,1)S(1)}, u32[]{:S(2)}, u32[]{:S(2)}) async-start(bf16[8,32,384]{2,1,0:T(8,128)(2,1)} %reshape.92), calls=%async_computation | async-start | bytes 393216 | tf_op jit(solution)/shard_map/all_to_all | solution.py:335
  24.7 1.2 %copy-start.1 = (f32[2,128,1536]{2,1,0:T(8,128)}, f32[2,128,1536]{2,1,0:T(8,128)S(1)}, u32[]{:S(2)}) copy-start(f32[2,128,1536]{2,1,0:T(8,128)S(1)} %get-tuple-element.56.refs_3_) | copy-start | bytes 4718596
  25.9 1.0 %copy-start.3 = (f32[2,128,1024]{2,1,0:T(8,128)}, f32[2,128,1024]{2,1,0:T(8,128)S(1)}, u32[]{:S(2)}) copy-start(f32[2,128,1024]{2,1,0:T(8,128)S(1)} %get-tuple-element.57.refs_4_) | copy-start | bytes 3145732
  27.8 17.6 %collective-permute-start.4 = (bf16[96,1024]{1,0:T(8,128)(2,1)S(1)}, bf16[96,1024]{1,0:T(8,128)(2,1)S(1)}, u32[]{:S(2)}, u32[]{:S(2)}) collective-permute-start(bf16[96,1024]{1,0:T(8,128)(2,1)S(1)} %collective-permute-done), channel_id=1, source_target_pairs={{0,1},{1,0},{2,3},{3,2},{4,5},{5,4},{6,7},{7,6},{8,9},{9,8},{10,11... | collective-permute-start | bytes 589832 | tf_op jit(solution)/shard_map/ppermute | solution.py:317
  29.7 15.7 %collective-permute-start.5 = (bf16[96,1024]{1,0:T(8,128)(2,1)S(1)}, bf16[96,1024]{1,0:T(8,128)(2,1)S(1)}, u32[]{:S(2)}, u32[]{:S(2)}) collective-permute-start(bf16[96,1024]{1,0:T(8,128)(2,1)S(1)} %collective-permute-done.1), channel_id=1, source_target_pairs={{0,1},{1,0},{2,3},{3,2},{4,5},{5,4},{6,7},{7,6},{8,9},{9,8},{10,11... | collective-permute-start | bytes 589832 | tf_op jit(solution)/shard_map/ppermute | solution.py:317
  29.8 16.9 %collective-permute-start.6 = (bf16[96,1024]{1,0:T(8,128)(2,1)S(1)}, bf16[96,1024]{1,0:T(8,128)(2,1)}, u32[]{:S(2)}, u32[]{:S(2)}) collective-permute-start(bf16[96,1024]{1,0:T(8,128)(2,1)S(1)} %collective-permute-done.2), channel_id=1, source_target_pairs={{0,1},{1,0},{2,3},{3,2},{4,5},{5,4},{6,7},{7,6},{8,9},{9,8},{10,11... | collective-permute-start | bytes 589832 | tf_op jit(solution)/shard_map/ppermute | solution.py:317
  31.7 19.3 %all-to-all-start.1 = ((bf16[8,264,128]{2,1,0:T(8,128)(2,1)}), bf16[8,264,128]{2,1,0:T(8,128)(2,1)S(1)}, u32[]{:S(2)}, u32[]{:S(2)}) async-start(bf16[8,264,128]{2,1,0:T(8,128)(2,1)} %pad_maximum_fusion), calls=%async_computation.1 | async-start | bytes 1081344 | tf_op jit(solution)/shard_map/all_to_all | solution.py:387
  45.4 0.7 copy-start.8
  46.0 0.7 copy-start.10
  46.7 0.9 %copy-start.9 = (bf16[96,1024]{1,0:T(8,128)(2,1)S(1)}, bf16[96,1024]{1,0:T(8,128)(2,1)}, u32[]{:S(2)}) copy-start(bf16[96,1024]{1,0:T(8,128)(2,1)} %copy-done.8) | copy-start | bytes 589828
  46.7 1.0 %copy-start.11 = (bf16[96,1024]{1,0:T(8,128)(2,1)S(1)}, bf16[96,1024]{1,0:T(8,128)(2,1)}, u32[]{:S(2)}) copy-start(bf16[96,1024]{1,0:T(8,128)(2,1)} %copy-done.10) | copy-start | bytes 589828
  48.7 2.4 %copy-start = (bf16[768,1024]{1,0:T(8,128)(2,1)}, bf16[768,1024]{1,0:T(8,128)(2,1)S(1)}, u32[]{:S(2)}) copy-start(bf16[768,1024]{1,0:T(8,128)(2,1)S(1)} %constant_dynamic-update-slice_fusion.refs_0_.part_ref) | copy-start | bytes 4718596
  49.5 26.6 %copy-start.2 = (bf16[1,64,1024]{2,1,0:T(8,128)(2,1)S(1)}, bf16[1,64,1024]{2,1,0:T(8,128)(2,1)}, u32[]{:S(2)}) copy-start(bf16[1,64,1024]{2,1,0:T(8,128)(2,1)} %param.16) | copy-start | bytes 393220
  49.5 15.5 %collective-permute-start.7 = (bf16[256,1024]{1,0:T(8,128)(2,1)S(1)}, bf16[256,1024]{1,0:T(8,128)(2,1)S(1)}, u32[]{:S(2)}, u32[]{:S(2)}) collective-permute-start(bf16[256,1024]{1,0:T(8,128)(2,1)S(1)} %place.1.refs_0_), channel_id=1, source_target_pairs={{0,16},{8,24},{16,0},{24,8},{1,17},{9,25},{17,1},{25,9},{2,18},{10... | collective-permute-start | bytes 1572872 | tf_op jit(solution)/shard_map/ppermute | solution.py:329
  51.1 0.8 %copy-start.5 = (bf16[8,264,128]{2,1,0:T(8,128)(2,1)}, bf16[8,264,128]{2,1,0:T(8,128)(2,1)S(1)}, u32[]{:S(2)}) copy-start(bf16[8,264,128]{2,1,0:T(8,128)(2,1)S(1)} %all-to-all-done.1.refs_2_) | copy-start | bytes 1622020
  59.2 17.0 %all-to-all-start.2 = ((bf16[8,192,128]{2,1,0:T(8,128)(2,1)}), bf16[8,192,128]{2,1,0:T(8,128)(2,1)S(1)}, u32[]{:S(2)}, u32[]{:S(2)}) async-start(bf16[8,192,128]{2,1,0:T(8,128)(2,1)} %attend.1), calls=%async_computation.2 | async-start | bytes 786432 | tf_op jit(solution)/shard_map/all_to_all | solution.py:426
  65.0 1.9 %collective-permute-start.8 = (bf16[256,1024]{1,0:T(8,128)(2,1)S(1)}, bf16[256,1024]{1,0:T(8,128)(2,1)S(1)}, u32[]{:S(2)}, u32[]{:S(2)}) collective-permute-start(bf16[256,1024]{1,0:T(8,128)(2,1)S(1)} %place.1.refs_0_), channel_id=1, source_target_pairs={{0,8},{8,0},{16,24},{24,16},{1,9},{9,1},{17,25},{25,17},{2,10},{10... | collective-permute-start | bytes 1572872 | tf_op jit(solution)/shard_map/ppermute | solution.py:331
  65.0 2.6 %collective-permute-start.9 = (bf16[256,1024]{1,0:T(8,128)(2,1)S(1)}, bf16[256,1024]{1,0:T(8,128)(2,1)S(1)}, u32[]{:S(2)}, u32[]{:S(2)}) collective-permute-start(bf16[256,1024]{1,0:T(8,128)(2,1)S(1)} %collective-permute-done.7.refs_1_), channel_id=1, source_target_pairs={{0,8},{8,0},{16,24},{24,16},{1,9},{9,1},{17,25},{25,17},{2,10},{10... | collective-permute-start | bytes 1572872 | tf_op jit(solution)/shard_map/ppermute | solution.py:331

commit v3 on v2

--- a/solution.py
+++ b/solution.py
@@ -12,7 +12,7 @@
 lanes = 128
 slot_base = 32
 mebibyte = 1024 * 1024
-vmem_grants = {"attend": 60 * mebibyte}
+vmem_grants = {"attend": 24 * mebibyte}
 vmem_grant = 16 * mebibyte
 
 
@@ -57,7 +57,7 @@
         copy.wait()
 
 
-def table_kernel(len_ref, bias_ref, bucket_ref, cache_out, new_out, cache_tab, new_tab, sems):
+def table_kernel(len_ref, bias_ref, bucket_ref, cache_tab, new_tab):
     heads, unused, reach = cache_tab.shape
     first_head = lax.axis_index("tok") * heads
     span = new_tab.shape[2]
@@ -71,7 +71,6 @@
     turned = jnp.dot(buckets, swap, preferred_element_type=jnp.float32).astype(jnp.int32)
     row = jnp.concatenate([turned[at : at + 1, :] for at in reversed(range(tiles))], axis=1)
     row = jnp.broadcast_to(row, (8, reach))
-    copies = []
     for h in range(heads):
         found = jnp.zeros((8, reach), jnp.float32)
         for bucket in range(bias_ref.shape[0]):
@@ -81,87 +80,78 @@
             pltpu.roll(found, len_ref[0] + (new_count - q_rows + 1), 1),
             pltpu.roll(jnp.concatenate([found[:, reach - new_count :], after], axis=1), span - q_rows + 1, 1),
         )
-        for at, (base, tab, out) in enumerate(
-            zip(bases, (cache_tab, new_tab), (cache_out, new_out))
-        ):
+        for base, tab in zip(bases, (cache_tab, new_tab)):
             sublane = lax.broadcasted_iota(jnp.int32, base.shape, 0)
             for bit in (1, 2, 4):
                 base = jnp.where((sublane & bit) != 0, pltpu.roll(base, bit, 1), base)
-            for group in range(q_rows // 8):
-                tab[h, group * 8 : (group + 1) * 8, :] = (
-                    pltpu.roll(base, group * 8, 1) if group else base
-                )
-            copy = pltpu.make_async_copy(tab.at[h], out.at[h], sems.at[2 * h + at])
-            copy.start()
-            copies.append(copy)
-    for copy in copies:
-        copy.wait()
-
-
-def attend_kernel(
-    near,
-    width,
-    head_size,
-    token_parts,
-    weight_parts,
-    len_ref,
-    *refs,
-):
-    x_refs = refs[:token_parts]
-    w_refs = refs[token_parts : token_parts + weight_parts]
-    (
-        cache_any,
-        cache_tab_any,
-        new_tab_any,
-        out_ref,
-        all_x,
-        all_w,
-        cache_ref,
-        cache_tab,
-        new_tab,
-        q_ref,
-        k_ref,
-        v_ref,
-        key_aug,
-        val_aug,
-        new_val_aug,
-        sems,
-    ) = refs[token_parts + weight_parts :]
-    head_count = width // head_size
-    peers = out_ref.shape[0]
-    tok_rows = out_ref.shape[1] // 3
-    new_count, full = q_ref.shape
-    cache_rows = (cache_ref.shape[1] - 8) // 2
-    cache_count = peers * cache_rows
-    length = len_ref[0]
+            tab[h] = base
+
+
+def project_kernel(near, x_any, w_any, out_ref, all_x, all_w, sems):
+    peers, width = lax.axis_size("tok"), w_any.shape[1]
+    parts, new_count, full = out_ref.shape
+    tok_rows, span = new_count // peers, x_any.shape[0] // peers
     pairs = [
         (
-            x_refs[0].at[pl.ds(at * (x_refs[0].shape[0] // peers), tok_rows)],
+            x_any.at[pl.ds(at * span, tok_rows)],
             all_x.at[pl.ds(pl.multiple_of(place * tok_rows, tok_rows), tok_rows)],
         )
         for at, place in enumerate(token_places(near))
     ]
-    pairs.append((w_refs[0], all_w))
-    first = len(pairs)
-    pairs += [(cache_any, cache_ref), (cache_tab_any, cache_tab), (new_tab_any, new_tab)]
-    copies = fetch(pairs, sems)
-    for copy in copies[:first]:
+    pairs.append((w_any, all_w))
+    for copy in fetch(pairs, sems):
         copy.wait()
-    made = jnp.dot(
-        all_x[...],
-        all_w[...],
-        preferred_element_type=jnp.float32,
-    ).astype(jnp.bfloat16)
-    for part, ref in enumerate((q_ref, k_ref, v_ref)):
+    depth = all_w.shape[0] // (parts * peers * lax.axis_size("fsdp"))
+    weights = all_w[...].reshape(-1, parts, depth, width)
+    weights = jnp.concatenate(
+        [weights[:, part].reshape(all_x.shape[1], width) for part in range(parts)], axis=1
+    )
+    made = jnp.dot(all_x[...], weights, preferred_element_type=jnp.float32).astype(jnp.bfloat16)
+    for part in range(parts):
         piece = made[:, part * width : (part + 1) * width]
         if width < full:
             piece = jnp.concatenate(
                 [piece, jnp.zeros((new_count, full - width), jnp.bfloat16)], axis=1
             )
-        ref[...] = piece
-
-    for copy in copies[first:]:
+        out_ref[part] = piece
+
+
+def attend_kernel(
+    width,
+    head_size,
+    len_ref,
+    made_any,
+    cache_any,
+    cache_base,
+    new_base,
+    out_ref,
+    made,
+    cache_ref,
+    cache_tab,
+    new_tab,
+    key_aug,
+    val_aug,
+    new_val_aug,
+    sems,
+):
+    head_count = width // head_size
+    peers = out_ref.shape[0]
+    tok_rows = out_ref.shape[1] // 3
+    new_count, full = made.shape[1:]
+    cache_rows = (cache_ref.shape[1] - 8) // 2
+    cache_count = peers * cache_rows
+    length = len_ref[0]
+    copies = fetch([(made_any, made), (cache_any, cache_ref)], sems)
+    for base_ref, tab in ((cache_base, cache_tab), (new_base, new_tab)):
+        for h in range(head_count):
+            for group in range(q_rows // 8):
+                tab[h, group * 8 : (group + 1) * 8, :] = (
+                    pltpu.roll(base_ref[h], group * 8, 1) if group else base_ref[h]
+                )
+    q_ref, k_ref, v_ref = (made.at[part] for part in range(3))
+    for copy in copies[:2]:
         copy.wait()
+
     told = cache_ref[:, 2 * cache_rows :, :].astype(jnp.float32)
     slots = jnp.concatenate(
         [
@@ -330,23 +320,22 @@
         swap = [(f, f ^ 1) for f in range(fsdp_count)]
         return parts + [lax.ppermute(one, "fsdp", swap) for one in parts]
 
-    sent_w = jnp.stack([w_query, w_key, w_value], axis=1).reshape(-1, 3, peers, width)
-    sent_w = jnp.transpose(sent_w, (2, 0, 1, 3)).reshape(peers, -1, 3 * width)
+    def columns(rows):
+        return jnp.transpose(rows.reshape(-1, peers, width), (1, 0, 2))
+
+    sent_w = jnp.concatenate([columns(w_query), columns(w_key), columns(w_value)], axis=1)
     got_w = lax.all_to_all(sent_w, "tok", split_axis=0, concat_axis=0, tiled=True)
 
     reach = bucket_table.shape[0]
-    shapes = [(my_heads, q_rows, reach), (my_heads, q_rows, 2 * new_count)]
     cache_tab, new_tab = call(
         table_kernel,
-        shapes,
+        [(my_heads, 8, reach), (my_heads, 8, 2 * new_count)],
         [smem()] * 2 + [vmem()],
-        [pltpu.VMEM(shape, jnp.float32) for shape in shapes]
-        + [pltpu.SemaphoreType.DMA((2 * my_heads,))],
+        [],
         "tables",
         0,
-        4 * my_heads * q_rows * (reach + 2 * new_count),
+        32 * my_heads * (reach + 2 * new_count),
         jnp.float32,
-        hbm,
     )(
         cache_len,
         rel_bias,
@@ -354,7 +343,7 @@
     )
 
     got_w, cache_tab, new_tab = lax.optimization_barrier((got_w, cache_tab, new_tab))
-    my_w = [lax.all_gather(got_w.reshape(-1, 3 * width), "fsdp", axis=0, tiled=True)]
+    my_w = [lax.all_gather(got_w.reshape(-1, width), "fsdp", axis=0, tiled=True)]
 
     wide_in = tokens.astype(jnp.float32)
     inverse = lax.rsqrt(jnp.mean(wide_in * wide_in, axis=-1, keepdims=True) + 1e-06)
@@ -368,9 +357,6 @@
     *parts, weights = lax.optimization_barrier((*parts, my_w[0]))
     my_w = [weights]
     parts = [jnp.concatenate(parts)]
-
-    def columns(rows):
-        return jnp.transpose(rows.reshape(-1, peers, width), (1, 0, 2))
 
     slots = token_slot[0]
     note = jnp.zeros((8, width), jnp.bfloat16)
@@ -399,29 +385,37 @@
 
     full = max(width, lanes)
     cache_count = peers * cache_rows
-    (sent,) = call(
-        functools.partial(attend_kernel, near, width, head_size, len(parts), len(my_w)),
-        [(peers, 3 * tok_rows, width)],
-        [smem()] + [hbm()] * (len(parts) + len(my_w) + 3),
+    (made,) = call(
+        functools.partial(project_kernel, near),
+        [(3, new_count, full)],
+        [hbm()] * 2,
         [
             pltpu.VMEM((new_count, features), jnp.bfloat16),
-            pltpu.VMEM((features, 3 * width), jnp.bfloat16),
+            pltpu.VMEM((3 * features, width), jnp.bfloat16),
+            pltpu.SemaphoreType.DMA((peers + 1,)),
+        ],
+        "project",
+        6 * new_count * features * width,
+        2 * features * (new_count + 3 * width),
+    )(*parts, *my_w)
+    (sent,) = call(
+        functools.partial(attend_kernel, width, head_size),
+        [(peers, 3 * tok_rows, width)],
+        [smem()] + [hbm()] * 2 + [vmem()] * 2,
+        [
+            pltpu.VMEM((3, new_count, full), jnp.bfloat16),
             pltpu.VMEM(cache.shape, jnp.bfloat16),
-            pltpu.VMEM(cache_tab.shape, jnp.float32),
-            pltpu.VMEM(new_tab.shape, jnp.float32),
-        ]
-        + [pltpu.VMEM((new_count, full), jnp.bfloat16)] * 3
-        + [
+            pltpu.VMEM((my_heads, q_rows, reach), jnp.float32),
+            pltpu.VMEM((my_heads, q_rows, 2 * new_count), jnp.float32),
             pltpu.VMEM((my_heads, cache_count, full), jnp.bfloat16),
             pltpu.VMEM((my_heads, cache_count, full), jnp.bfloat16),
             pltpu.VMEM((my_heads, new_count, full), jnp.bfloat16),
-            pltpu.SemaphoreType.DMA((peers + len(my_w) + 3,)),
+            pltpu.SemaphoreType.DMA((2,)),
         ],
         "attend",
-        6 * new_count * features * width
-        + 4 * my_heads * new_count * (new_count + cache_count) * full,
-        2 * features * (new_count + 3 * width) + 4 * full * cache_count,
-    )(cache_len, *parts, *my_w, cache, cache_tab, new_tab)
+        4 * my_heads * new_count * (new_count + cache_count) * full,
+        8 * full * cache_count,
+    )(cache_len, made, cache, cache_tab, new_tab)
 
     got = lax.all_to_all(sent, "tok", split_axis=0, concat_axis=0, tiled=True)
     hidden, new_keys, new_values = call(

time: 78.2 us -> 73.2 us (0.936)
  local copies, waits for them, and re-layouts: 10.9 us -> 2.83 us
  waiting for transfers between devices: 10.6 us -> 17.6 us
  starting transfers between devices: 28.4 us -> 26.1 us
  Pallas kernels: 12.8 us -> 11.3 us
    unnamed x41 -> x24, local copies, waits for them, and re-layouts: 8.33 us -> 0.56 us
    all_to_all x1, waiting for transfers between devices: 0.01 us -> 4.58 us  [shards(): lax.all_to_all(sent_w, 'tok', split_axis=0, concat_axis=0, tiled=True)]
    transpose x0 -> x2, local copies, waits for them, and re-layouts: none -> 1.72 us  [columns(): return jnp.transpose(rows.reshape(-1, peers, width), (1, 0, 2))]
    all_to_all x1, waiting for transfers between devices: 0.01 us -> 1.64 us  [shards(): lax.all_to_all(sent_cache, 'tok', split_axis=0, concat_axis=0, tiled=True)]
    all_to_all x1, starting transfers between devices: 5.86 us -> 4.4 us  [shards(): got = lax.all_to_all(sent, 'tok', split_axis=0, concat_axis=0, tiled=True)]
    pallas_call x2 -> x3, Pallas kernels: 10.5 us -> 9.09 us  [the longest x1 5.46 us: shards(): call(functools.partial(attend_kernel, width, head_size), [(peers, 3 * tok...]
    ppermute x1, starting transfers between devices: 1.56 us -> 0.6 us  [gather_fsdp(): parts.append(lax.ppermute(part, 'fsdp', turn))]
    concatenate x1, local copies, waits for them, and re-layouts: 0.94 us -> 0.02 us  [shards(): parts = [jnp.concatenate(parts)]]
  transfers between devices with their start and end apart: 13 -> 13, of which waited for: 3 -> 5; matrix products, arithmetic and copies ran while one was open for 9% -> 6% of each run, Pallas kernels for 15% -> 14%
where the time goes in v3:
time: 73.2 us; the launch traced here: 72.6 us
  starting transfers between devices  26.1 us (36%)
  waiting for transfers between devices  17.6 us (24%)
  Pallas kernels  11.3 us (15%)
  blocking collectives  8.58 us (12%)
  other arithmetic  4.54 us (6%)
  local copies, waits for them, and re-layouts  2.83 us (4%)
  between operations  1.59 us (2%)
    all_to_all x1, waiting for transfers between devices, shards(): got = lax.all_to_all(sent, 'tok', split_axis=0, concat_axis=0, tiled=True)  9.24 us
    all_gather x1, blocking collectives, shards(): lax.all_gather(got_w.reshape(-1, width), 'fsdp', axis=0, tiled=True)  8.58 us
    ppermute x3, starting transfers between devices, shards(): lax.ppermute(normed, 'tok', far_turn(step))  7.01 us
    ppermute x4, starting transfers between devices, over_tok(): return [lax.ppermute(part, 'tok', turns) for part in parts]  5.46 us
    pallas_call x1, Pallas kernels, shards(): call(functools.partial(attend_kernel, width, head_size), [(peers, 3 * tok...  5.46 us
    all_to_all x1, starting transfers between devices, shards(): lax.all_to_all(sent_cache, 'tok', split_axis=0, concat_axis=0, tiled=True)  4.77 us
    all_to_all x1, waiting for transfers between devices, shards(): lax.all_to_all(sent_w, 'tok', split_axis=0, concat_axis=0, tiled=True)  4.58 us
    all_to_all x1, starting transfers between devices, shards(): got = lax.all_to_all(sent, 'tok', split_axis=0, concat_axis=0, tiled=True)  4.4 us
  transfers between devices with their start and end apart: 13, of which 5 were waited for; matrix products, arithmetic and copies ran while one was open for 6% of the time, Pallas kernels for 14%

profile of v3, /device:TPU:0, one launch (start us, length us, event | category | flops | bytes accessed | tf_op | source)
XLA Modules:
  0.0 72.6 jit_solution(5323745249146813558)
XLA Ops:
  0.6 0.0 copy-start
  0.7 1.1 %fusion = f32[64]{0:T(128)S(1)} fusion(bf16[1,64,1024]{2,1,0:T(8,128)(2,1)} %param.16), kind=kLoop, calls=%fused_computation.3 | loop fusion | flops 196544 | bytes 131328 | tf_op jit(solution)/shard_map/reduce_sum | solution.py:349
  1.8 1.0 %fusion.2 = bf16[64,1024]{1,0:T(8,128)(2,1)S(1)} fusion(f32[1024]{0:T(1024)} %param.23, f32[64]{0:T(128)S(1)} %add_rsqrt_fusion, bf16[1,64,1024]{2,1,0:T(8,128)(2,1)} %param.16), kind=kLoop, calls=%fused_computation.5 | loop fusion | flops 262144 | bytes 266496 | tf_op jit(solution)/shard_map/convert_element_type | solution.py:350
  2.8 0.9 %pad_maximum_fusion.1 = bf16[96,1024]{1,0:T(8,128)(2,1)S(1)} fusion(bf16[32,1024]{1,0:T(8,128)(2,1)} %param.27, bf16[64,1024]{1,0:T(8,128)(2,1)S(1)} %fusion.2), kind=kLoop, calls=%fused_computation.6 | loop fusion | flops 393216 | bytes 393216 | tf_op jit(solution)/shard_map/concatenate | solution.py:352
  3.7 3.1 %collective-permute-start = (bf16[96,1024]{1,0:T(8,128)(2,1)S(1)}, bf16[96,1024]{1,0:T(8,128)(2,1)S(1)}, u32[]{:S(2)}, u32[]{:S(2)}) collective-permute-start(bf16[96,1024]{1,0:T(8,128)(2,1)S(1)} %pad_maximum_fusion.1), channel_id=1, source_target_pairs={{0,2},{1,3},{2,4},{3,5},{4,6},{5,7},{6,0},{7,1},{8,10},{9,11},{10,... | collective-permute-start | bytes 589832 | tf_op jit(solution)/shard_map/ppermute | solution.py:353
  6.8 2.6 %collective-permute-start.1 = (bf16[96,1024]{1,0:T(8,128)(2,1)S(1)}, bf16[96,1024]{1,0:T(8,128)(2,1)S(1)}, u32[]{:S(2)}, u32[]{:S(2)}) collective-permute-start(bf16[96,1024]{1,0:T(8,128)(2,1)S(1)} %pad_maximum_fusion.1), channel_id=1, source_target_pairs={{0,4},{1,5},{2,6},{3,7},{4,0},{5,1},{6,2},{7,3},{8,12},{9,13},{10,... | collective-permute-start | bytes 589832 | tf_op jit(solution)/shard_map/ppermute | solution.py:353
  9.4 1.3 %collective-permute-start.2 = (bf16[96,1024]{1,0:T(8,128)(2,1)S(1)}, bf16[96,1024]{1,0:T(8,128)(2,1)S(1)}, u32[]{:S(2)}, u32[]{:S(2)}) collective-permute-start(bf16[96,1024]{1,0:T(8,128)(2,1)S(1)} %pad_maximum_fusion.1), channel_id=1, source_target_pairs={{0,6},{1,7},{2,0},{3,1},{4,2},{5,3},{6,4},{7,5},{8,14},{9,15},{10,... | collective-permute-start | bytes 589832 | tf_op jit(solution)/shard_map/ppermute | solution.py:353
  10.7 1.5 %collective-permute-start.3 = (bf16[96,1024]{1,0:T(8,128)(2,1)S(1)}, bf16[96,1024]{1,0:T(8,128)(2,1)S(1)}, u32[]{:S(2)}, u32[]{:S(2)}) collective-permute-start(bf16[96,1024]{1,0:T(8,128)(2,1)S(1)} %pad_maximum_fusion.1), channel_id=1, source_target_pairs={{0,1},{1,0},{2,3},{3,2},{4,5},{5,4},{6,7},{7,6},{8,9},{9,8},{10,11... | collective-permute-start | bytes 589832 | tf_op jit(solution)/shard_map/ppermute | solution.py:307
  12.2 0.9 %bitcast_bitcast_fusion.2 = bf16[8,32,128]{2,1,0:T(8,128)(2,1)S(1)} fusion(bf16[32,1024]{1,0:T(8,128)(2,1)} %param.24), kind=kLoop, calls=%fused_computation.10 | loop fusion | bytes 131072 | tf_op jit(solution)/shard_map/transpose | solution.py:324
  13.1 0.0 copy-start.2
  13.1 0.9 %bitcast_bitcast_fusion = (bf16[8,32,128]{2,1,0:T(8,128)(2,1)S(1)}, bf16[8,32,128]{2,1,0:T(8,128)(2,1)S(1)}) fusion(bf16[32,1024]{1,0:T(8,128)(2,1)S(1)} %copy-done, bf16[32,1024]{1,0:T(8,128)(2,1)} %param.26), kind=kLoop, calls=%fused_computation.8 | loop fusion | bytes 262144 | tf_op jit(solution)/shard_map/transpose | solution.py:324
  14.0 0.7 pad_maximum_fusion.2
  14.7 3.4 %all-to-all-start = ((bf16[8,96,128]{2,1,0:T(8,128)(2,1)}), bf16[8,96,128]{2,1,0:T(8,128)(2,1)S(1)}, u32[]{:S(2)}, u32[]{:S(2)}) async-start(bf16[8,96,128]{2,1,0:T(8,128)(2,1)} %pad_maximum_fusion.2), calls=%async_computation | async-start | bytes 393216 | tf_op jit(solution)/shard_map/all_to_all | solution.py:327
  18.7 0.1 copy.22.bias_ref
  18.8 0.2 copy.23
  19.0 0.2 copy.24
  19.2 0.2 copy.25
  19.4 0.2 copy.26
  19.6 1.5 %tables.1 = (f32[2,8,1536]{2,1,0:T(8,128)S(1)}, f32[2,8,1024]{2,1,0:T(8,128)S(1)}) custom-call(s32[1]{0:T(128)S(6)} %copy.41.len_ref, f32[32,16]{1,0:T(8,128)S(1)} %copy.22.bias_ref, s32[12,128]{1,0:T(8,128)S(1)} %bitcast.34), custom_call_target="tpu_custom_call" | custom-call | bytes 163840 | tf_op jit(solution)/shard_map/tables/pallas_call | solution.py:330
  21.1 0.2 scatter.9
  21.2 0.8 %pad_maximum_fusion = bf16[8,264,128]{2,1,0:T(8,128)(2,1)} fusion(bf16[8,8,128]{2,1,0:T(8,128)(2,1)S(1)} %broadcast_in_dim.8, bf16[8,128,128]{2,1,0:T(8,128)(2,1)S(1)} %bitcast.38, bf16[8,128,128]{2,1,0:T(8,128)(2,1)S(1)} %bitcast.37), kind=kLoop, calls=%fused_computation | loop fusion | flops 1622016 | bytes 1081344 | tf_op jit(solution)/shard_map/concatenate | solution.py:365
  22.1 0.0 collective-permute-done
  22.1 1.9 %collective-permute-start.4 = (bf16[96,1024]{1,0:T(8,128)(2,1)S(1)}, bf16[96,1024]{1,0:T(8,128)(2,1)S(1)}, u32[]{:S(2)}, u32[]{:S(2)}) collective-permute-start(bf16[96,1024]{1,0:T(8,128)(2,1)S(1)} %collective-permute-done), channel_id=1, source_target_pairs={{0,1},{1,0},{2,3},{3,2},{4,5},{5,4},{6,7},{7,6},{8,9},{9,8},{10,11... | collective-permute-start | bytes 589832 | tf_op jit(solution)/shard_map/ppermute | solution.py:307
  24.0 0.0 collective-permute-done.1
  24.0 0.2 collective-permute-start.5
  24.2 0.0 collective-permute-done.2
  24.2 1.9 %collective-permute-start.6 = (bf16[96,1024]{1,0:T(8,128)(2,1)S(1)}, bf16[96,1024]{1,0:T(8,128)(2,1)S(1)}, u32[]{:S(2)}, u32[]{:S(2)}) collective-permute-start(bf16[96,1024]{1,0:T(8,128)(2,1)S(1)} %collective-permute-done.2), channel_id=1, source_target_pairs={{0,1},{1,0},{2,3},{3,2},{4,5},{5,4},{6,7},{7,6},{8,9},{9,8},{10,11... | collective-permute-start | bytes 589832 | tf_op jit(solution)/shard_map/ppermute | solution.py:307
  26.0 4.6 %all-to-all-done = bf16[8,96,128]{2,1,0:T(8,128)(2,1)S(1)} async-done(((bf16[8,96,128]{2,1,0:T(8,128)(2,1)}), bf16[8,96,128]{2,1,0:T(8,128)(2,1)S(1)}, u32[]{:S(2)}, u32[]{:S(2)}) %all-to-all-start) | async-done | bytes 196640 | tf_op jit(solution)/shard_map/all_to_all | solution.py:327
  30.6 4.8 %all-to-all-start.1 = ((bf16[8,264,128]{2,1,0:T(8,128)(2,1)}), bf16[8,264,128]{2,1,0:T(8,128)(2,1)S(1)}, u32[]{:S(2)}, u32[]{:S(2)}) async-start(bf16[8,264,128]{2,1,0:T(8,128)(2,1)} %pad_maximum_fusion), calls=%async_computation.1 | async-start | bytes 1081344 | tf_op jit(solution)/shard_map/all_to_all | solution.py:373
  35.4 8.6 %all_gather.3.w_any = bf16[3072,128]{1,0:T(8,128)(2,1)S(1)} all-gather(bf16[768,128]{1,0:T(8,128)(2,1)S(1)} %bitcast.39), channel_id=1, replica_groups=mesh['fsdp'=4,'tok'=8] {'fsdp'}, dimensions={0}, use_global_device_ids=true | all-gather | bytes 983040 | tf_op jit(solution)/shard_map/all_gather | solution.py:346
  44.0 0.0 collective-permute-done.3
  44.0 0.0 collective-permute-done.4
  44.0 0.0 collective-permute-done.5
  44.0 0.0 collective-permute-done.6
  44.2 0.8 %place.1.refs_0_ = bf16[256,1024]{1,0:T(8,128)(2,1)S(1)} custom-call(bf16[768,1024]{1,0:T(8,128)(2,1)S(1)} %constant_dynamic-update-slice_fusion.x_any.part_ref), custom_call_target="tpu_custom_call" | custom-call | bytes 1048576 | tf_op jit(solution)/shard_map/place/pallas_call | solution.py:375
  45.0 0.6 collective-permute-start.7
  45.6 2.2 %project.1.made_any = bf16[3,512,128]{2,1,0:T(8,128)(2,1)S(1)} custom-call(bf16[768,1024]{1,0:T(8,128)(2,1)S(1)} %constant_dynamic-update-slice_fusion.x_any.part_ref, bf16[3072,128]{1,0:T(8,128)(2,1)S(1)} %all_gather.3.w_any), custom_call_target="tpu_custom_call" | custom-call | flops 402653184 | bytes 1835008 | tf_op jit(solution)/shard_map/project/pallas_call | solution.py:388
  47.8 0.0 copy-start.1
  47.8 1.6 %all-to-all-done.1.cache_any = bf16[8,264,128]{2,1,0:T(8,128)(2,1)S(1)} async-done(((bf16[8,264,128]{2,1,0:T(8,128)(2,1)}), bf16[8,264,128]{2,1,0:T(8,128)(2,1)S(1)}, u32[]{:S(2)}, u32[]{:S(2)}) %all-to-all-start.1) | async-done | bytes 540704 | tf_op jit(solution)/shard_map/all_to_all | solution.py:373
  49.4 5.5 %attend.1 = bf16[8,192,128]{2,1,0:T(8,128)(2,1)} custom-call(s32[1]{0:T(128)S(6)} %copy.41.len_ref, bf16[3,512,128]{2,1,0:T(8,128)(2,1)S(1)} %project.1.made_any, bf16[8,264,128]{2,1,0:T(8,128)(2,1)S(1)} %all-to-all-done.1.cache_any, f32[2,8,1536]{2,1,0:T(8,128)S(1)} %get-tuple-element.56.cache_base, f32[2,8,1024]{2,1,0:T(8,128)S(1)} %get-tuple-element.57.new_base), custom_call_target="tpu_custom_call" | custom-call | flops 805306368 | bytes 1048576 | tf_op jit(solution)/shard_map/attend/pallas_call | solution.py:401
  54.9 4.4 %all-to-all-start.2 = ((bf16[8,192,128]{2,1,0:T(8,128)(2,1)}), bf16[8,192,128]{2,1,0:T(8,128)(2,1)S(1)}, u32[]{:S(2)}, u32[]{:S(2)}) async-start(bf16[8,192,128]{2,1,0:T(8,128)(2,1)} %attend.1), calls=%async_computation.2 | async-start | bytes 786432 | tf_op jit(solution)/shard_map/all_to_all | solution.py:420
  59.3 0.0 collective-permute-start.8
  59.3 0.0 collective-permute-done.7.refs_1_
  59.3 0.5 collective-permute-start.9
  59.8 1.4 %collective-permute-done.8.refs_2_ = bf16[256,1024]{1,0:T(8,128)(2,1)S(1)} collective-permute-done((bf16[256,1024]{1,0:T(8,128)(2,1)S(1)}, bf16[256,1024]{1,0:T(8,128)(2,1)S(1)}, u32[]{:S(2)}, u32[]{:S(2)}) %collective-permute-start.8) | collective-permute-done | bytes 524320 | tf_op jit(solution)/shard_map/ppermute | solution.py:321
  61.2 0.7 %collective-permute-done.9.refs_3_ = bf16[256,1024]{1,0:T(8,128)(2,1)S(1)} collective-permute-done((bf16[256,1024]{1,0:T(8,128)(2,1)S(1)}, bf16[256,1024]{1,0:T(8,128)(2,1)S(1)}, u32[]{:S(2)}, u32[]{:S(2)}) %collective-permute-start.9) | collective-permute-done | bytes 524320 | tf_op jit(solution)/shard_map/ppermute | solution.py:321
  61.9 9.2 %all-to-all-done.2.got_ref = bf16[8,192,128]{2,1,0:T(8,128)(2,1)S(1)} async-done(((bf16[8,192,128]{2,1,0:T(8,128)(2,1)}), bf16[8,192,128]{2,1,0:T(8,128)(2,1)S(1)}, u32[]{:S(2)}, u32[]{:S(2)}) %all-to-all-start.2) | async-done | bytes 393248 | tf_op jit(solution)/shard_map/all_to_all | solution.py:420
  71.2 1.4 %finish.1 = (bf16[64,1024]{1,0:T(8,128)(2,1)}, bf16[64,1024]{1,0:T(8,128)(2,1)}, bf16[64,1024]{1,0:T(8,128)(2,1)}) custom-call(bf16[8,192,128]{2,1,0:T(8,128)(2,1)S(1)} %all-to-all-done.2.got_ref, bf16[64,1024]{1,0:T(8,128)(2,1)S(1)} %bitcast.33, bf16[256,1024]{1,0:T(8,128)(2,1)S(1)} %place.1.refs_0_, bf16[256,1024]{1,0:T(8,128)(2,1)S(1)} %collective-permute-done.7.refs_1_, ...), custom_call_target="tpu_custom_call" | custom-call | flops 134217728 | bytes 2752512 | tf_op jit(solution)/shard_map/finish/pallas_call | solution.py:421
  (23 shorter events, 0.2 us)
Async XLA Ops:
  0.6 12.4 %copy-start = (bf16[32,1024]{1,0:T(8,128)(2,1)S(1)}, bf16[32,1024]{1,0:T(8,128)(2,1)}, u32[]{:S(2)}) copy-start(bf16[32,1024]{1,0:T(8,128)(2,1)} %param.25) | copy-start | bytes 196612
  0.6 17.4 %copy-start.6 = (s32[1,64]{1,0:T(1,128)S(1)}, s32[1,64]{1,0:T(1,128)}, u32[]{:S(2)}) copy-start(s32[1,64]{1,0:T(1,128)} %param.20) | copy-start | bytes 772
  0.7 18.1 %copy-start.5 = (f32[32,16]{0,1:T(8,128)S(1)}, f32[32,16]{0,1:T(8,128)}, u32[]{:S(2)}) copy-start(f32[32,16]{0,1:T(8,128)} %param.22) | copy-start | bytes 6148
  0.7 18.2 %copy-start.3 = (bf16[1,128,1024]{2,1,0:T(8,128)(2,1)S(1)}, bf16[1,128,1024]{2,1,0:T(8,128)(2,1)}, u32[]{:S(2)}) copy-start(bf16[1,128,1024]{2,1,0:T(8,128)(2,1)} %param.17) | copy-start | bytes 786436
  0.7 18.5 %copy-start.4 = (bf16[1,128,1024]{2,1,0:T(8,128)(2,1)S(1)}, bf16[1,128,1024]{2,1,0:T(8,128)(2,1)}, u32[]{:S(2)}) copy-start(bf16[1,128,1024]{2,1,0:T(8,128)(2,1)} %param.18) | copy-start | bytes 786436
  3.7 18.4 %collective-permute-start = (bf16[96,1024]{1,0:T(8,128)(2,1)S(1)}, bf16[96,1024]{1,0:T(8,128)(2,1)S(1)}, u32[]{:S(2)}, u32[]{:S(2)}) collective-permute-start(bf16[96,1024]{1,0:T(8,128)(2,1)S(1)} %pad_maximum_fusion.1), channel_id=1, source_target_pairs={{0,2},{1,3},{2,4},{3,5},{4,6},{5,7},{6,0},{7,1},{8,10},{9,11},{10,... | collective-permute-start | bytes 589832 | tf_op jit(solution)/shard_map/ppermute | solution.py:353
  6.8 17.2 %collective-permute-start.1 = (bf16[96,1024]{1,0:T(8,128)(2,1)S(1)}, bf16[96,1024]{1,0:T(8,128)(2,1)S(1)}, u32[]{:S(2)}, u32[]{:S(2)}) collective-permute-start(bf16[96,1024]{1,0:T(8,128)(2,1)S(1)} %pad_maximum_fusion.1), channel_id=1, source_target_pairs={{0,4},{1,5},{2,6},{3,7},{4,0},{5,1},{6,2},{7,3},{8,12},{9,13},{10,... | collective-permute-start | bytes 589832 | tf_op jit(solution)/shard_map/ppermute | solution.py:353
  9.4 14.8 %collective-permute-start.2 = (bf16[96,1024]{1,0:T(8,128)(2,1)S(1)}, bf16[96,1024]{1,0:T(8,128)(2,1)S(1)}, u32[]{:S(2)}, u32[]{:S(2)}) collective-permute-start(bf16[96,1024]{1,0:T(8,128)(2,1)S(1)} %pad_maximum_fusion.1), channel_id=1, source_target_pairs={{0,6},{1,7},{2,0},{3,1},{4,2},{5,3},{6,4},{7,5},{8,14},{9,15},{10,... | collective-permute-start | bytes 589832 | tf_op jit(solution)/shard_map/ppermute | solution.py:353
  10.7 33.3 %collective-permute-start.3 = (bf16[96,1024]{1,0:T(8,128)(2,1)S(1)}, bf16[96,1024]{1,0:T(8,128)(2,1)S(1)}, u32[]{:S(2)}, u32[]{:S(2)}) collective-permute-start(bf16[96,1024]{1,0:T(8,128)(2,1)S(1)} %pad_maximum_fusion.1), channel_id=1, source_target_pairs={{0,1},{1,0},{2,3},{3,2},{4,5},{5,4},{6,7},{7,6},{8,9},{9,8},{10,11... | collective-permute-start | bytes 589832 | tf_op jit(solution)/shard_map/ppermute | solution.py:307
  13.1 6.5 %copy-start.2 = (s32[1536]{0:T(1024)S(1)}, s32[1536]{0:T(1024)}, u32[]{:S(2)}) copy-start(s32[1536]{0:T(1024)} %param.21) | copy-start | bytes 18436
  14.7 15.9 %all-to-all-start = ((bf16[8,96,128]{2,1,0:T(8,128)(2,1)}), bf16[8,96,128]{2,1,0:T(8,128)(2,1)S(1)}, u32[]{:S(2)}, u32[]{:S(2)}) async-start(bf16[8,96,128]{2,1,0:T(8,128)(2,1)} %pad_maximum_fusion.2), calls=%async_computation | async-start | bytes 393216 | tf_op jit(solution)/shard_map/all_to_all | solution.py:327
  22.1 21.9 %collective-permute-start.4 = (bf16[96,1024]{1,0:T(8,128)(2,1)S(1)}, bf16[96,1024]{1,0:T(8,128)(2,1)S(1)}, u32[]{:S(2)}, u32[]{:S(2)}) collective-permute-start(bf16[96,1024]{1,0:T(8,128)(2,1)S(1)} %collective-permute-done), channel_id=1, source_target_pairs={{0,1},{1,0},{2,3},{3,2},{4,5},{5,4},{6,7},{7,6},{8,9},{9,8},{10,11... | collective-permute-start | bytes 589832 | tf_op jit(solution)/shard_map/ppermute | solution.py:307
  24.0 20.0 %collective-permute-start.5 = (bf16[96,1024]{1,0:T(8,128)(2,1)S(1)}, bf16[96,1024]{1,0:T(8,128)(2,1)S(1)}, u32[]{:S(2)}, u32[]{:S(2)}) collective-permute-start(bf16[96,1024]{1,0:T(8,128)(2,1)S(1)} %collective-permute-done.1), channel_id=1, source_target_pairs={{0,1},{1,0},{2,3},{3,2},{4,5},{5,4},{6,7},{7,6},{8,9},{9,8},{10,11... | collective-permute-start | bytes 589832 | tf_op jit(solution)/shard_map/ppermute | solution.py:307
  24.2 19.8 %collective-permute-start.6 = (bf16[96,1024]{1,0:T(8,128)(2,1)S(1)}, bf16[96,1024]{1,0:T(8,128)(2,1)S(1)}, u32[]{:S(2)}, u32[]{:S(2)}) collective-permute-start(bf16[96,1024]{1,0:T(8,128)(2,1)S(1)} %collective-permute-done.2), channel_id=1, source_target_pairs={{0,1},{1,0},{2,3},{3,2},{4,5},{5,4},{6,7},{7,6},{8,9},{9,8},{10,11... | collective-permute-start | bytes 589832 | tf_op jit(solution)/shard_map/ppermute | solution.py:307
  30.6 18.8 %all-to-all-start.1 = ((bf16[8,264,128]{2,1,0:T(8,128)(2,1)}), bf16[8,264,128]{2,1,0:T(8,128)(2,1)S(1)}, u32[]{:S(2)}, u32[]{:S(2)}) async-start(bf16[8,264,128]{2,1,0:T(8,128)(2,1)} %pad_maximum_fusion), calls=%async_computation.1 | async-start | bytes 1081344 | tf_op jit(solution)/shard_map/all_to_all | solution.py:373
  45.0 14.3 %collective-permute-start.7 = (bf16[256,1024]{1,0:T(8,128)(2,1)S(1)}, bf16[256,1024]{1,0:T(8,128)(2,1)S(1)}, u32[]{:S(2)}, u32[]{:S(2)}) collective-permute-start(bf16[256,1024]{1,0:T(8,128)(2,1)S(1)} %place.1.refs_0_), channel_id=1, source_target_pairs={{0,16},{8,24},{16,0},{24,8},{1,17},{9,25},{17,1},{25,9},{2,18},{10... | collective-permute-start | bytes 1572872 | tf_op jit(solution)/shard_map/ppermute | solution.py:319
  47.8 23.4 %copy-start.1 = (bf16[1,64,1024]{2,1,0:T(8,128)(2,1)S(1)}, bf16[1,64,1024]{2,1,0:T(8,128)(2,1)}, u32[]{:S(2)}) copy-start(bf16[1,64,1024]{2,1,0:T(8,128)(2,1)} %param.16) | copy-start | bytes 393220
  54.9 16.3 %all-to-all-start.2 = ((bf16[8,192,128]{2,1,0:T(8,128)(2,1)}), bf16[8,192,128]{2,1,0:T(8,128)(2,1)S(1)}, u32[]{:S(2)}, u32[]{:S(2)}) async-start(bf16[8,192,128]{2,1,0:T(8,128)(2,1)} %attend.1), calls=%async_computation.2 | async-start | bytes 786432 | tf_op jit(solution)/shard_map/all_to_all | solution.py:420
  59.3 1.9 %collective-permute-start.8 = (bf16[256,1024]{1,0:T(8,128)(2,1)S(1)}, bf16[256,1024]{1,0:T(8,128)(2,1)S(1)}, u32[]{:S(2)}, u32[]{:S(2)}) collective-permute-start(bf16[256,1024]{1,0:T(8,128)(2,1)S(1)} %place.1.refs_0_), channel_id=1, source_target_pairs={{0,8},{8,0},{16,24},{24,16},{1,9},{9,1},{17,25},{25,17},{2,10},{10... | collective-permute-start | bytes 1572872 | tf_op jit(solution)/shard_map/ppermute | solution.py:321
  59.3 2.6 %collective-permute-start.9 = (bf16[256,1024]{1,0:T(8,128)(2,1)S(1)}, bf16[256,1024]{1,0:T(8,128)(2,1)S(1)}, u32[]{:S(2)}, u32[]{:S(2)}) collective-permute-start(bf16[256,1024]{1,0:T(8,128)(2,1)S(1)} %collective-permute-done.7.refs_1_), channel_id=1, source_target_pairs={{0,8},{8,0},{16,24},{24,16},{1,9},{9,1},{17,25},{25,17},{2,10},{10... | collective-permute-start | bytes 1572872 | tf_op jit(solution)/shard_map/ppermute | solution.py:321

commit v4 on v3

--- a/solution.py
+++ b/solution.py
@@ -12,7 +12,7 @@
 lanes = 128
 slot_base = 32
 mebibyte = 1024 * 1024
-vmem_grants = {"attend": 24 * mebibyte}
+vmem_grants = {"attend": 24 * mebibyte, "open": 60 * mebibyte}
 vmem_grant = 16 * mebibyte
 
 
@@ -26,15 +26,21 @@
     return copies
 
 
-def token_places(near):
-    peers, me = lax.axis_size("tok"), lax.axis_index("tok")
-    far_of = [lax.rem(me + peers - near * step, peers) for step in range(peers // near)]
-    places = list(far_of)
-    for turn in range(1, near):
-        places += [
-            one - lax.rem(one, near) + lax.rem(one + near - turn, near) for one in far_of
-        ]
-    return places
+def tok_turns(count):
+    turns = []
+    bit = count // 2
+    while bit:
+        turns.append(bit)
+        bit //= 2
+    return turns
+
+
+def token_places():
+    masks = [0]
+    for turn in tok_turns(lax.axis_size("tok")):
+        masks += [mask + turn for mask in masks]
+    me = lax.axis_index("tok")
+    return [lax.bitwise_xor(me, jnp.int32(mask)) for mask in masks]
 
 
 def fsdp_origins():
@@ -43,8 +49,29 @@
     return origins + [origin + 1 - 2 * lax.rem(origin, 2) for origin in origins]
 
 
-def place_kernel(near, part_ref, out_ref, sems):
-    places = token_places(near)
+def open_kernel(
+    gain_ref, states_any, wq_any, wk_any, wv_any, wo_any, block_ref, out_ref, tokens, weights, sems
+):
+    peers, unused, width = out_ref.shape
+    rows, depth = tokens.shape[0], weights.shape[1]
+    sources = [(states_any.at[0], tokens), (wo_any, block_ref.at[rows:])]
+    sources += [(any_ref, weights.at[at]) for at, any_ref in enumerate((wq_any, wk_any, wv_any))]
+    copies = fetch(sources, sems)
+    copies[0].wait()
+    wide = tokens[...].astype(jnp.float32)
+    inverse = lax.rsqrt(jnp.mean(wide * wide, axis=-1, keepdims=True) + 1e-06)
+    block_ref[:rows, :] = (wide * inverse * gain_ref[...]).astype(jnp.bfloat16)
+    for part in range(3):
+        copies[2 + part].wait()
+        for dest in range(peers):
+            out_ref[dest, part * depth : (part + 1) * depth, :] = weights[
+                part, :, dest * width : (dest + 1) * width
+            ]
+    copies[1].wait()
+
+
+def place_kernel(part_ref, out_ref, sems):
+    places = token_places()
     rows, span = out_ref.shape[0] // len(places), part_ref.shape[0] // len(places)
     pairs = [
         (
@@ -87,7 +114,7 @@
             tab[h] = base
 
 
-def project_kernel(near, x_any, w_any, out_ref, all_x, all_w, sems):
+def project_kernel(x_any, w_any, out_ref, all_x, all_w, sems):
     peers, width = lax.axis_size("tok"), w_any.shape[1]
     parts, new_count, full = out_ref.shape
     tok_rows, span = new_count // peers, x_any.shape[0] // peers
@@ -96,7 +123,7 @@
             x_any.at[pl.ds(at * span, tok_rows)],
             all_x.at[pl.ds(pl.multiple_of(place * tok_rows, tok_rows), tok_rows)],
         )
-        for at, place in enumerate(token_places(near))
+        for at, place in enumerate(token_places())
     ]
     pairs.append((w_any, all_w))
     for copy in fetch(pairs, sems):
@@ -189,43 +216,51 @@
         new_val_aug[h] = jnp.where(mine_new, v_ref[...], one)
 
     lane = lax.broadcasted_iota(jnp.int32, (q_rows, full), 1)
-    per_dest = tok_rows
-    for block in range(new_count // q_rows):
-        q_here = q_ref[block * q_rows : (block + 1) * q_rows, :]
-        start = new_count - q_rows - block * q_rows
-        seen = (block + 1) * q_rows
-        made = None
+    turn_lhs = (((1,), (1,)), ((), ()))
+    group = min(2, new_count // q_rows)
+    for first in range(0, new_count // q_rows, group):
+        blocks = range(first, first + group)
+        q_here = [q_ref[block * q_rows : (block + 1) * q_rows, :] for block in blocks]
+        made_here = [None] * group
         for h in range(head_count):
             spare = ((h + 1) * head_size) % full
             mine = (lane >= h * head_size) & (lane < (h + 1) * head_size)
-            q_new = jnp.where(mine, q_here, jnp.zeros((), jnp.bfloat16))
-            q_old = jnp.where(lane == spare, one, q_new)
-            s_old = lax.dot_general(
-                q_old, key_aug[h], (((1,), (1,)), ((), ())), preferred_element_type=jnp.float32
+            q_new = [jnp.where(mine, q, jnp.zeros((), jnp.bfloat16)) for q in q_here]
+            q_old = jnp.concatenate([jnp.where(lane == spare, one, q) for q in q_new])
+            s_all = lax.dot_general(
+                q_old, key_aug[h], turn_lhs, preferred_element_type=jnp.float32
             )
-            s_new = lax.dot_general(
-                q_new,
-                k_ref[:seen, :],
-                (((1,), (1,)), ((), ())),
-                preferred_element_type=jnp.float32,
+            p_all, fresh = [], []
+            for at, block in enumerate(blocks):
+                start = new_count - q_rows - block * q_rows
+                seen = (block + 1) * q_rows
+                s_old = s_all[at * q_rows : (at + 1) * q_rows]
+                s_old = s_old + cache_tab[h, :, start : start + cache_count]
+                s_new = lax.dot_general(
+                    q_new[at], k_ref[:seen, :], turn_lhs, preferred_element_type=jnp.float32
+                )
+                s_new = s_new + new_tab[h, :, start : start + seen]
+                peak = jnp.maximum(
+                    jnp.max(s_old, axis=1, keepdims=True), jnp.max(s_new, axis=1, keepdims=True)
+                )
+                p_all.append(jnp.exp(s_old - peak).astype(jnp.bfloat16))
+                p_new = jnp.exp(s_new - peak).astype(jnp.bfloat16)
+                fresh.append(
+                    jnp.dot(p_new, new_val_aug[h, :seen, :], preferred_element_type=jnp.float32)
+                )
+            totals = jnp.dot(
+                jnp.concatenate(p_all), val_aug[h], preferred_element_type=jnp.float32
             )
-            s_old = s_old + cache_tab[h, :, start : start + cache_count]
-            s_new = s_new + new_tab[h, :, start : start + seen]
-            peak = jnp.maximum(
-                jnp.max(s_old, axis=1, keepdims=True), jnp.max(s_new, axis=1, keepdims=True)
-            )
-            p_old = jnp.exp(s_old - peak).astype(jnp.bfloat16)
-            p_new = jnp.exp(s_new - peak).astype(jnp.bfloat16)
-            total = jnp.dot(p_old, val_aug[h], preferred_element_type=jnp.float32) + jnp.dot(
-                p_new, new_val_aug[h, :seen, :], preferred_element_type=jnp.float32
-            )
-            part = total / total[:, spare : spare + 1]
-            made = part if made is None else jnp.where(mine, part, made)
-        made = made.astype(jnp.bfloat16)
-        for piece in range(q_rows // per_dest):
-            out_ref[block * (q_rows // per_dest) + piece, :per_dest, :] = made[
-                piece * per_dest : (piece + 1) * per_dest, :width
-            ]
+            for at in range(group):
+                total = totals[at * q_rows : (at + 1) * q_rows] + fresh[at]
+                part = total / total[:, spare : spare + 1]
+                made_here[at] = part if h == 0 else jnp.where(mine, part, made_here[at])
+        for block, ready in zip(blocks, made_here):
+            ready = ready.astype(jnp.bfloat16)
+            for piece in range(q_rows // tok_rows):
+                out_ref[block * (q_rows // tok_rows) + piece, :tok_rows, :] = ready[
+                    piece * tok_rows : (piece + 1) * tok_rows, :width
+                ]
 
 
 def finish_kernel(got_ref, states_ref, *refs):
@@ -276,7 +311,6 @@
 
 
 def shards(
-    near,
     states,
     cache_keys,
     cache_values,
@@ -301,16 +335,6 @@
     cache_rows = cache_keys.shape[1]
 
     fsdp_count = lax.axis_size("fsdp")
-    far = peers // near
-
-    def over_tok(parts, turns):
-        return [lax.ppermute(part, "tok", turns) for part in parts]
-
-    def far_turn(step):
-        return [(t, (t + near * step) % peers) for t in range(peers)]
-
-    def near_turn(step):
-        return [(t, t - t % near + (t + step) % near) for t in range(peers)]
 
     def gather_fsdp(part):
         parts = [part]
@@ -323,8 +347,23 @@
     def columns(rows):
         return jnp.transpose(rows.reshape(-1, peers, width), (1, 0, 2))
 
-    sent_w = jnp.concatenate([columns(w_query), columns(w_key), columns(w_value)], axis=1)
+    depth, out_rows = w_query.shape[0], w_out.shape[0]
+    block, sent_w = call(
+        open_kernel,
+        [(tok_rows + out_rows, features), (peers, 3 * depth, width)],
+        [vmem()] + [hbm()] * 5,
+        [
+            pltpu.VMEM((tok_rows, features), jnp.bfloat16),
+            pltpu.VMEM((3, depth, features), jnp.bfloat16),
+            pltpu.SemaphoreType.DMA((5,)),
+        ],
+        "open",
+        0,
+        14 * features * depth,
+    )(norm_gain.reshape(1, features), states, w_query, w_key, w_value, w_out)
     got_w = lax.all_to_all(sent_w, "tok", split_axis=0, concat_axis=0, tiled=True)
+
+    my_w = [lax.all_gather(got_w.reshape(-1, width), "fsdp", axis=0, tiled=True)]
 
     reach = bucket_table.shape[0]
     cache_tab, new_tab = call(
@@ -342,22 +381,6 @@
         bucket_table.reshape(reach // lanes, lanes),
     )
 
-    got_w, cache_tab, new_tab = lax.optimization_barrier((got_w, cache_tab, new_tab))
-    my_w = [lax.all_gather(got_w.reshape(-1, width), "fsdp", axis=0, tiled=True)]
-
-    wide_in = tokens.astype(jnp.float32)
-    inverse = lax.rsqrt(jnp.mean(wide_in * wide_in, axis=-1, keepdims=True) + 1e-06)
-    normed = (wide_in * inverse * norm_gain).astype(jnp.bfloat16)
-    out_rows = w_out.shape[0]
-    normed = jnp.concatenate([normed, w_out])
-    parts = [normed] + [lax.ppermute(normed, "tok", far_turn(step)) for step in range(1, far)]
-    for turn in range(1, near):
-        parts += over_tok(parts[:far], near_turn(turn))
-
-    *parts, weights = lax.optimization_barrier((*parts, my_w[0]))
-    my_w = [weights]
-    parts = [jnp.concatenate(parts)]
-
     slots = token_slot[0]
     note = jnp.zeros((8, width), jnp.bfloat16)
     note = note.at[0, :tok_rows].set((slots // slot_base).astype(jnp.bfloat16))
@@ -370,10 +393,24 @@
         ],
         axis=1,
     )
+
+    parts = [block]
+    for turn in tok_turns(peers):
+        pairs = [(t, t ^ turn) for t in range(peers)]
+        parts += [lax.ppermute(part, "tok", pairs) for part in parts]
+        if len(parts) == 2:
+            parts[1], cache_tab, new_tab = lax.optimization_barrier(
+                (parts[1], cache_tab, new_tab)
+            )
+
+    *parts, weights = lax.optimization_barrier((*parts, my_w[0]))
+    my_w = [weights]
+    parts = [jnp.concatenate(parts)]
+
     cache = lax.all_to_all(sent_cache, "tok", split_axis=0, concat_axis=0, tiled=True)
 
     (out_tok,) = call(
-        functools.partial(place_kernel, near),
+        place_kernel,
         [(peers * out_rows, features)],
         [hbm()],
         [pltpu.SemaphoreType.DMA((peers,))],
@@ -386,7 +423,7 @@
     full = max(width, lanes)
     cache_count = peers * cache_rows
     (made,) = call(
-        functools.partial(project_kernel, near),
+        project_kernel,
         [(3, new_count, full)],
         [hbm()] * 2,
         [
@@ -450,9 +487,8 @@
         P(("fsdp", "tok"), None),
     )
     out_specs = (P("fsdp", "tok", None), P("fsdp", "tok", None), P("fsdp", "tok", None))
-    near = 2 if mesh.shape["tok"] <= 8 else 4
     return jax.shard_map(
-        functools.partial(shards, near),
+        shards,
         mesh=mesh,
         in_specs=in_specs,
         out_specs=out_specs,

time: 73.2 us -> 68.4 us (0.934)
  waiting for transfers between devices: 17.6 us -> 10.3 us
  other arithmetic: 4.54 us -> 1.52 us
  starting transfers between devices: 26.1 us -> 28.9 us
  Pallas kernels: 11.3 us -> 13.5 us
    all_to_all x1, waiting for transfers between devices: 4.58 us -> 0.01 us  [shards(): lax.all_to_all(sent_w, 'tok', split_axis=0, concat_axis=0, tiled=True)]
    pallas_call x2 -> x3, Pallas kernels: 2.98 us -> 5.56 us  [the longest x1 2.61 us: shards(): call(open_kernel, [(tok_rows + out_rows, features), (peers, 3 * depth, wi...]
    unnamed x24 -> x18, local copies, waits for them, and re-layouts: 0.56 us -> 2.87 us
    all_to_all x1, starting transfers between devices: 4.4 us -> 6.15 us  [shards(): got = lax.all_to_all(sent, 'tok', split_axis=0, concat_axis=0, tiled=True)]
    transpose x2 -> x0, local copies, waits for them, and re-layouts: 1.72 us -> none  [columns(): return jnp.transpose(rows.reshape(-1, peers, width), (1, 0, 2))]
    all_to_all x1, waiting for transfers between devices: 1.64 us -> 0.01 us  [shards(): lax.all_to_all(sent_cache, 'tok', split_axis=0, concat_axis=0, tiled=True)]
    all_to_all x1, waiting for transfers between devices: 9.24 us -> 7.68 us  [shards(): got = lax.all_to_all(sent, 'tok', split_axis=0, concat_axis=0, tiled=True)]
    concatenate x2 -> x0, other arithmetic: 1.55 us -> none  [the longest x1 0.86 us: shards(): normed = jnp.concatenate([normed, w_out])]
  transfers between devices with their start and end apart: 13 -> 13, of which waited for: 5 -> 3; matrix products, arithmetic and copies ran while one was open for 6% -> 6% of each run, Pallas kernels for 14% -> 14%
where the time goes in v4:
time: 68.4 us; the launch traced here: 67.9 us
  starting transfers between devices  28.9 us (42%)
  Pallas kernels  13.5 us (20%)
  waiting for transfers between devices  10.3 us (15%)
  blocking collectives  8.58 us (13%)
  local copies, waits for them, and re-layouts  3.42 us (5%)
  other arithmetic  1.52 us (2%)
  between operations  1.51 us (2%)
    ppermute x7, starting transfers between devices, shards(): parts += [lax.ppermute(part, 'tok', pairs) for part in parts]  12.7 us
    all_gather x1, blocking collectives, shards(): lax.all_gather(got_w.reshape(-1, width), 'fsdp', axis=0, tiled=True)  8.58 us
    all_to_all x1, waiting for transfers between devices, shards(): got = lax.all_to_all(sent, 'tok', split_axis=0, concat_axis=0, tiled=True)  7.68 us
    all_to_all x1, starting transfers between devices, shards(): got = lax.all_to_all(sent, 'tok', split_axis=0, concat_axis=0, tiled=True)  6.15 us
    pallas_call x1, Pallas kernels, shards(): call(functools.partial(attend_kernel, width, head_size), [(peers, 3 * tok...  5.1 us
    all_to_all x1, starting transfers between devices, shards(): lax.all_to_all(sent_cache, 'tok', split_axis=0, concat_axis=0, tiled=True)  4.65 us
    all_to_all x1, starting transfers between devices, shards(): lax.all_to_all(sent_w, 'tok', split_axis=0, concat_axis=0, tiled=True)  3.39 us
    unnamed x18, local copies, waits for them, and re-layouts  2.87 us
  transfers between devices with their start and end apart: 13, of which 3 were waited for; matrix products, arithmetic and copies ran while one was open for 6% of the time, Pallas kernels for 14%

profile of v4, /device:TPU:0, one launch (start us, length us, event | category | flops | bytes accessed | tf_op | source)
XLA Modules:
  0.0 67.9 jit_solution(2785180215268627700)
XLA Ops:
  0.6 0.0 copy-start.2
  0.6 2.6 %open.1 = (bf16[96,1024]{1,0:T(8,128)(2,1)}, bf16[8,96,128]{2,1,0:T(8,128)(2,1)}) custom-call(f32[1,1024]{1,0:T(1,128)} %bitcast.18, bf16[1,64,1024]{2,1,0:T(8,128)(2,1)} %states_any.1, bf16[32,1024]{1,0:T(8,128)(2,1)} %wq_any.1, bf16[32,1024]{1,0:T(8,128)(2,1)} %wk_any.1, bf16[32,1024]{1,0:T(8,128)(2,1)} %wv_any.1, bf16[32,1024]{1,0:T(8,128)(2,1)} %wo_any.1), custom_call_target="tpu_custom_call" | custom-call | bytes 458752 | tf_op jit(solution)/shard_map/open/pallas_call | solution.py:351
  3.3 4.1 %collective-permute-start = (bf16[96,1024]{1,0:T(8,128)(2,1)}, bf16[96,1024]{1,0:T(8,128)(2,1)S(1)}, u32[]{:S(2)}, u32[]{:S(2)}) collective-permute-start(bf16[96,1024]{1,0:T(8,128)(2,1)} %get-tuple-element.51), channel_id=1, source_target_pairs={{0,4},{1,5},{2,6},{3,7},{4,0},{5,1},{6,2},{7,3},{8,12},{9,13},{10,... | collective-permute-start | bytes 589832 | tf_op jit(solution)/shard_map/ppermute | solution.py:400
  7.4 1.6 %collective-permute-start.1 = (bf16[96,1024]{1,0:T(8,128)(2,1)}, bf16[96,1024]{1,0:T(8,128)(2,1)S(1)}, u32[]{:S(2)}, u32[]{:S(2)}) collective-permute-start(bf16[96,1024]{1,0:T(8,128)(2,1)} %get-tuple-element.51), channel_id=1, source_target_pairs={{0,2},{1,3},{2,0},{3,1},{4,6},{5,7},{6,4},{7,5},{8,10},{9,11},{10,... | collective-permute-start | bytes 589832 | tf_op jit(solution)/shard_map/ppermute | solution.py:400
  8.9 1.5 %collective-permute-start.3 = (bf16[96,1024]{1,0:T(8,128)(2,1)}, bf16[96,1024]{1,0:T(8,128)(2,1)S(1)}, u32[]{:S(2)}, u32[]{:S(2)}) collective-permute-start(bf16[96,1024]{1,0:T(8,128)(2,1)} %get-tuple-element.51), channel_id=1, source_target_pairs={{0,1},{1,0},{2,3},{3,2},{4,5},{5,4},{6,7},{7,6},{8,9},{9,8},{10,11... | collective-permute-start | bytes 589832 | tf_op jit(solution)/shard_map/ppermute | solution.py:400
  10.5 3.4 %all-to-all-start = ((bf16[8,96,128]{2,1,0:T(8,128)(2,1)}), bf16[8,96,128]{2,1,0:T(8,128)(2,1)S(1)}, u32[]{:S(2)}, u32[]{:S(2)}) async-start(bf16[8,96,128]{2,1,0:T(8,128)(2,1)} %get-tuple-element.50), calls=%async_computation | async-start | bytes 393216 | tf_op jit(solution)/shard_map/all_to_all | solution.py:364
  14.5 0.8 %copy.16.bias_ref = f32[32,16]{1,0:T(8,128)S(1)} copy(f32[32,16]{0,1:T(8,128)} %param.22) | data formatting | bytes 4096 | tf_op args[6]
  15.3 0.7 %copy-done.1 = s32[1536]{0:T(1024)S(1)} copy-done((s32[1536]{0:T(1024)S(1)}, s32[1536]{0:T(1024)}, u32[]{:S(2)}) %copy-start.1) | copy-done | bytes 6168
  16.0 1.5 %tables.1 = (f32[2,8,1536]{2,1,0:T(8,128)S(1)}, f32[2,8,1024]{2,1,0:T(8,128)S(1)}) custom-call(s32[1]{0:T(128)S(6)} %copy.29.len_ref, f32[32,16]{1,0:T(8,128)S(1)} %copy.16.bias_ref, s32[12,128]{1,0:T(8,128)S(1)} %bitcast.12), custom_call_target="tpu_custom_call" | custom-call | bytes 163840 | tf_op jit(solution)/shard_map/tables/pallas_call | solution.py:369
  17.4 0.0 collective-permute-done
  17.4 2.0 %collective-permute-start.2 = (bf16[96,1024]{1,0:T(8,128)(2,1)S(1)}, bf16[96,1024]{1,0:T(8,128)(2,1)S(1)}, u32[]{:S(2)}, u32[]{:S(2)}) collective-permute-start(bf16[96,1024]{1,0:T(8,128)(2,1)S(1)} %collective-permute-done), channel_id=1, source_target_pairs={{0,2},{1,3},{2,0},{3,1},{4,6},{5,7},{6,4},{7,5},{8,10},{9,11},{10,... | collective-permute-start | bytes 589832 | tf_op jit(solution)/shard_map/ppermute | solution.py:400
  19.4 0.7 fusion
  20.1 1.1 %copy.17 = bf16[1,128,1024]{1,2,0:T(8,128)(2,1)S(1)} copy(bf16[1,128,1024]{2,1,0:T(8,128)(2,1)} %param.17) | data formatting | bytes 524288 | tf_op args[1]
  21.2 0.2 copy.18
  21.4 0.0 copy-done.2
  21.4 0.2 copy.19
  21.6 0.2 copy.20
  21.8 0.2 scatter.9
  22.0 0.0 copy-start.3
  22.0 0.9 %pad_maximum_fusion = bf16[8,264,128]{2,1,0:T(8,128)(2,1)} fusion(bf16[8,8,128]{2,1,0:T(8,128)(2,1)S(1)} %broadcast_in_dim.16, bf16[8,128,128]{2,1,0:T(8,128)(2,1)S(1)} %bitcast.16, bf16[8,128,128]{2,1,0:T(8,128)(2,1)S(1)} %bitcast.15), kind=kLoop, calls=%fused_computation | loop fusion | flops 1622016 | bytes 1081344 | tf_op jit(solution)/shard_map/concatenate | solution.py:388
  22.8 1.5 %collective-permute-start.4 = (bf16[96,1024]{1,0:T(8,128)(2,1)S(1)}, bf16[96,1024]{1,0:T(8,128)(2,1)S(1)}, u32[]{:S(2)}, u32[]{:S(2)}) collective-permute-start(bf16[96,1024]{1,0:T(8,128)(2,1)S(1)} %collective-permute-done), channel_id=1, source_target_pairs={{0,1},{1,0},{2,3},{3,2},{4,5},{5,4},{6,7},{7,6},{8,9},{9,8},{10,11... | collective-permute-start | bytes 589832 | tf_op jit(solution)/shard_map/ppermute | solution.py:400
  24.3 0.0 collective-permute-done.1
  24.3 0.5 collective-permute-start.5
  24.9 0.0 collective-permute-done.2
  24.9 1.5 %collective-permute-start.6 = (bf16[96,1024]{1,0:T(8,128)(2,1)S(1)}, bf16[96,1024]{1,0:T(8,128)(2,1)S(1)}, u32[]{:S(2)}, u32[]{:S(2)}) collective-permute-start(bf16[96,1024]{1,0:T(8,128)(2,1)S(1)} %collective-permute-done.2), channel_id=1, source_target_pairs={{0,1},{1,0},{2,3},{3,2},{4,5},{5,4},{6,7},{7,6},{8,9},{9,8},{10,11... | collective-permute-start | bytes 589832 | tf_op jit(solution)/shard_map/ppermute | solution.py:400
  26.4 0.0 all-to-all-done
  26.4 4.7 %all-to-all-start.1 = ((bf16[8,264,128]{2,1,0:T(8,128)(2,1)}), bf16[8,264,128]{2,1,0:T(8,128)(2,1)S(1)}, u32[]{:S(2)}, u32[]{:S(2)}) async-start(bf16[8,264,128]{2,1,0:T(8,128)(2,1)} %pad_maximum_fusion), calls=%async_computation.1 | async-start | bytes 1081344 | tf_op jit(solution)/shard_map/all_to_all | solution.py:410
  31.0 8.6 %all_gather.3.w_any = bf16[3072,128]{1,0:T(8,128)(2,1)S(1)} all-gather(bf16[768,128]{1,0:T(8,128)(2,1)S(1)} %bitcast.17), channel_id=1, replica_groups=mesh['fsdp'=4,'tok'=8] {'fsdp'}, dimensions={0}, use_global_device_ids=true | all-gather | bytes 983040 | tf_op jit(solution)/shard_map/all_gather | solution.py:366
  39.6 0.0 collective-permute-done.3
  39.6 0.0 collective-permute-done.4
  39.6 0.0 collective-permute-done.5
  39.6 1.2 %collective-permute-done.6 = bf16[96,1024]{1,0:T(8,128)(2,1)S(1)} collective-permute-done((bf16[96,1024]{1,0:T(8,128)(2,1)S(1)}, bf16[96,1024]{1,0:T(8,128)(2,1)S(1)}, u32[]{:S(2)}, u32[]{:S(2)}) %collective-permute-start.6) | collective-permute-done | bytes 196640 | tf_op jit(solution)/shard_map/ppermute | solution.py:400
  40.9 0.0 copy-done.3
  41.0 0.8 %place.1.refs_0_ = bf16[256,1024]{1,0:T(8,128)(2,1)S(1)} custom-call(bf16[768,1024]{1,0:T(8,128)(2,1)S(1)} %constant_dynamic-update-slice_fusion.x_any.part_ref), custom_call_target="tpu_custom_call" | custom-call | bytes 1048576 | tf_op jit(solution)/shard_map/place/pallas_call | solution.py:412
  41.8 1.6 %collective-permute-start.7 = (bf16[256,1024]{1,0:T(8,128)(2,1)S(1)}, bf16[256,1024]{1,0:T(8,128)(2,1)S(1)}, u32[]{:S(2)}, u32[]{:S(2)}) collective-permute-start(bf16[256,1024]{1,0:T(8,128)(2,1)S(1)} %place.1.refs_0_), channel_id=1, source_target_pairs={{0,16},{8,24},{16,0},{24,8},{1,17},{9,25},{17,1},{25,9},{2,18},{10... | collective-permute-start | bytes 1572872 | tf_op jit(solution)/shard_map/ppermute | solution.py:343
  43.4 2.2 %project.1.made_any = bf16[3,512,128]{2,1,0:T(8,128)(2,1)S(1)} custom-call(bf16[768,1024]{1,0:T(8,128)(2,1)S(1)} %constant_dynamic-update-slice_fusion.x_any.part_ref, bf16[3072,128]{1,0:T(8,128)(2,1)S(1)} %all_gather.3.w_any), custom_call_target="tpu_custom_call" | custom-call | flops 402653184 | bytes 1835008 | tf_op jit(solution)/shard_map/project/pallas_call | solution.py:425
  45.6 0.0 copy-start
  45.6 0.0 all-to-all-done.1.cache_any
  45.6 5.1 %attend.1 = bf16[8,192,128]{2,1,0:T(8,128)(2,1)} custom-call(s32[1]{0:T(128)S(6)} %copy.29.len_ref, bf16[3,512,128]{2,1,0:T(8,128)(2,1)S(1)} %project.1.made_any, bf16[8,264,128]{2,1,0:T(8,128)(2,1)S(1)} %all-to-all-done.1.cache_any, f32[2,8,1536]{2,1,0:T(8,128)S(1)} %get-tuple-element.60.cache_base, f32[2,8,1024]{2,1,0:T(8,128)S(1)} %get-tuple-element.61.new_base), custom_call_target="tpu_custom_call" | custom-call | flops 805306368 | bytes 1048576 | tf_op jit(solution)/shard_map/attend/pallas_call | solution.py:438
  50.7 6.1 %all-to-all-start.2 = ((bf16[8,192,128]{2,1,0:T(8,128)(2,1)}), bf16[8,192,128]{2,1,0:T(8,128)(2,1)S(1)}, u32[]{:S(2)}, u32[]{:S(2)}) async-start(bf16[8,192,128]{2,1,0:T(8,128)(2,1)} %attend.1), calls=%async_computation.2 | async-start | bytes 786432 | tf_op jit(solution)/shard_map/all_to_all | solution.py:457
  56.8 0.0 collective-permute-start.8
  56.8 0.0 collective-permute-done.7.refs_1_
  56.9 0.5 collective-permute-start.9
  57.4 1.4 %collective-permute-done.8.refs_2_ = bf16[256,1024]{1,0:T(8,128)(2,1)S(1)} collective-permute-done((bf16[256,1024]{1,0:T(8,128)(2,1)S(1)}, bf16[256,1024]{1,0:T(8,128)(2,1)S(1)}, u32[]{:S(2)}, u32[]{:S(2)}) %collective-permute-start.8) | collective-permute-done | bytes 524320 | tf_op jit(solution)/shard_map/ppermute | solution.py:345
  58.7 7.7 %all-to-all-done.2.got_ref = bf16[8,192,128]{2,1,0:T(8,128)(2,1)S(1)} async-done(((bf16[8,192,128]{2,1,0:T(8,128)(2,1)}), bf16[8,192,128]{2,1,0:T(8,128)(2,1)S(1)}, u32[]{:S(2)}, u32[]{:S(2)}) %all-to-all-start.2) | async-done | bytes 393248 | tf_op jit(solution)/shard_map/all_to_all | solution.py:457
  66.4 0.0 collective-permute-done.9.refs_3_
  66.4 0.0 copy-done
  66.4 1.4 %finish.1 = (bf16[64,1024]{1,0:T(8,128)(2,1)}, bf16[64,1024]{1,0:T(8,128)(2,1)}, bf16[64,1024]{1,0:T(8,128)(2,1)}) custom-call(bf16[8,192,128]{2,1,0:T(8,128)(2,1)S(1)} %all-to-all-done.2.got_ref, bf16[64,1024]{1,0:T(8,128)(2,1)S(1)} %bitcast.11, bf16[256,1024]{1,0:T(8,128)(2,1)S(1)} %place.1.refs_0_, bf16[256,1024]{1,0:T(8,128)(2,1)S(1)} %collective-permute-done.7.refs_1_, ...), custom_call_target="tpu_custom_call" | custom-call | flops 134217728 | bytes 2752512 | tf_op jit(solution)/shard_map/finish/pallas_call | solution.py:458
  (11 shorter events, 0.1 us)
Async XLA Ops:
  0.6 20.8 %copy-start.2 = (bf16[1,128,1024]{2,1,0:T(8,128)(2,1)S(1)}, bf16[1,128,1024]{2,1,0:T(8,128)(2,1)}, u32[]{:S(2)}) copy-start(bf16[1,128,1024]{2,1,0:T(8,128)(2,1)} %param.18) | copy-start | bytes 786436
  3.3 14.2 %collective-permute-start = (bf16[96,1024]{1,0:T(8,128)(2,1)}, bf16[96,1024]{1,0:T(8,128)(2,1)S(1)}, u32[]{:S(2)}, u32[]{:S(2)}) collective-permute-start(bf16[96,1024]{1,0:T(8,128)(2,1)} %get-tuple-element.51), channel_id=1, source_target_pairs={{0,4},{1,5},{2,6},{3,7},{4,0},{5,1},{6,2},{7,3},{8,12},{9,13},{10,... | collective-permute-start | bytes 589832 | tf_op jit(solution)/shard_map/ppermute | solution.py:400
  7.4 17.0 %collective-permute-start.1 = (bf16[96,1024]{1,0:T(8,128)(2,1)}, bf16[96,1024]{1,0:T(8,128)(2,1)S(1)}, u32[]{:S(2)}, u32[]{:S(2)}) collective-permute-start(bf16[96,1024]{1,0:T(8,128)(2,1)} %get-tuple-element.51), channel_id=1, source_target_pairs={{0,2},{1,3},{2,0},{3,1},{4,6},{5,7},{6,4},{7,5},{8,10},{9,11},{10,... | collective-permute-start | bytes 589832 | tf_op jit(solution)/shard_map/ppermute | solution.py:400
  8.9 30.7 %collective-permute-start.3 = (bf16[96,1024]{1,0:T(8,128)(2,1)}, bf16[96,1024]{1,0:T(8,128)(2,1)S(1)}, u32[]{:S(2)}, u32[]{:S(2)}) collective-permute-start(bf16[96,1024]{1,0:T(8,128)(2,1)} %get-tuple-element.51), channel_id=1, source_target_pairs={{0,1},{1,0},{2,3},{3,2},{4,5},{5,4},{6,7},{7,6},{8,9},{9,8},{10,11... | collective-permute-start | bytes 589832 | tf_op jit(solution)/shard_map/ppermute | solution.py:400
  10.5 15.9 %all-to-all-start = ((bf16[8,96,128]{2,1,0:T(8,128)(2,1)}), bf16[8,96,128]{2,1,0:T(8,128)(2,1)S(1)}, u32[]{:S(2)}, u32[]{:S(2)}) async-start(bf16[8,96,128]{2,1,0:T(8,128)(2,1)} %get-tuple-element.50), calls=%async_computation | async-start | bytes 393216 | tf_op jit(solution)/shard_map/all_to_all | solution.py:364
  15.3 0.7 %copy-start.1 = (s32[1536]{0:T(1024)S(1)}, s32[1536]{0:T(1024)}, u32[]{:S(2)}) copy-start(s32[1536]{0:T(1024)} %param.21) | copy-start | bytes 18436
  17.4 7.4 %collective-permute-start.2 = (bf16[96,1024]{1,0:T(8,128)(2,1)S(1)}, bf16[96,1024]{1,0:T(8,128)(2,1)S(1)}, u32[]{:S(2)}, u32[]{:S(2)}) collective-permute-start(bf16[96,1024]{1,0:T(8,128)(2,1)S(1)} %collective-permute-done), channel_id=1, source_target_pairs={{0,2},{1,3},{2,0},{3,1},{4,6},{5,7},{6,4},{7,5},{8,10},{9,11},{10,... | collective-permute-start | bytes 589832 | tf_op jit(solution)/shard_map/ppermute | solution.py:400
  22.0 18.9 %copy-start.3 = (bf16[96,1024]{1,0:T(8,128)(2,1)S(1)}, bf16[96,1024]{1,0:T(8,128)(2,1)}, u32[]{:S(2)}) copy-start(bf16[96,1024]{1,0:T(8,128)(2,1)} %get-tuple-element.51) | copy-start | bytes 589828
  22.8 16.8 %collective-permute-start.4 = (bf16[96,1024]{1,0:T(8,128)(2,1)S(1)}, bf16[96,1024]{1,0:T(8,128)(2,1)S(1)}, u32[]{:S(2)}, u32[]{:S(2)}) collective-permute-start(bf16[96,1024]{1,0:T(8,128)(2,1)S(1)} %collective-permute-done), channel_id=1, source_target_pairs={{0,1},{1,0},{2,3},{3,2},{4,5},{5,4},{6,7},{7,6},{8,9},{9,8},{10,11... | collective-permute-start | bytes 589832 | tf_op jit(solution)/shard_map/ppermute | solution.py:400
  24.3 15.3 %collective-permute-start.5 = (bf16[96,1024]{1,0:T(8,128)(2,1)S(1)}, bf16[96,1024]{1,0:T(8,128)(2,1)S(1)}, u32[]{:S(2)}, u32[]{:S(2)}) collective-permute-start(bf16[96,1024]{1,0:T(8,128)(2,1)S(1)} %collective-permute-done.1), channel_id=1, source_target_pairs={{0,1},{1,0},{2,3},{3,2},{4,5},{5,4},{6,7},{7,6},{8,9},{9,8},{10,11... | collective-permute-start | bytes 589832 | tf_op jit(solution)/shard_map/ppermute | solution.py:400
  24.9 16.0 %collective-permute-start.6 = (bf16[96,1024]{1,0:T(8,128)(2,1)S(1)}, bf16[96,1024]{1,0:T(8,128)(2,1)S(1)}, u32[]{:S(2)}, u32[]{:S(2)}) collective-permute-start(bf16[96,1024]{1,0:T(8,128)(2,1)S(1)} %collective-permute-done.2), channel_id=1, source_target_pairs={{0,1},{1,0},{2,3},{3,2},{4,5},{5,4},{6,7},{7,6},{8,9},{9,8},{10,11... | collective-permute-start | bytes 589832 | tf_op jit(solution)/shard_map/ppermute | solution.py:400
  26.4 19.2 %all-to-all-start.1 = ((bf16[8,264,128]{2,1,0:T(8,128)(2,1)}), bf16[8,264,128]{2,1,0:T(8,128)(2,1)S(1)}, u32[]{:S(2)}, u32[]{:S(2)}) async-start(bf16[8,264,128]{2,1,0:T(8,128)(2,1)} %pad_maximum_fusion), calls=%async_computation.1 | async-start | bytes 1081344 | tf_op jit(solution)/shard_map/all_to_all | solution.py:410
  41.8 15.0 %collective-permute-start.7 = (bf16[256,1024]{1,0:T(8,128)(2,1)S(1)}, bf16[256,1024]{1,0:T(8,128)(2,1)S(1)}, u32[]{:S(2)}, u32[]{:S(2)}) collective-permute-start(bf16[256,1024]{1,0:T(8,128)(2,1)S(1)} %place.1.refs_0_), channel_id=1, source_target_pairs={{0,16},{8,24},{16,0},{24,8},{1,17},{9,25},{17,1},{25,9},{2,18},{10... | collective-permute-start | bytes 1572872 | tf_op jit(solution)/shard_map/ppermute | solution.py:343
  45.6 20.9 %copy-start = (bf16[1,64,1024]{2,1,0:T(8,128)(2,1)S(1)}, bf16[1,64,1024]{2,1,0:T(8,128)(2,1)}, u32[]{:S(2)}) copy-start(bf16[1,64,1024]{2,1,0:T(8,128)(2,1)} %states_any.1) | copy-start | bytes 393220
  50.7 15.7 %all-to-all-start.2 = ((bf16[8,192,128]{2,1,0:T(8,128)(2,1)}), bf16[8,192,128]{2,1,0:T(8,128)(2,1)S(1)}, u32[]{:S(2)}, u32[]{:S(2)}) async-start(bf16[8,192,128]{2,1,0:T(8,128)(2,1)} %attend.1), calls=%async_computation.2 | async-start | bytes 786432 | tf_op jit(solution)/shard_map/all_to_all | solution.py:457
  56.8 1.9 %collective-permute-start.8 = (bf16[256,1024]{1,0:T(8,128)(2,1)S(1)}, bf16[256,1024]{1,0:T(8,128)(2,1)S(1)}, u32[]{:S(2)}, u32[]{:S(2)}) collective-permute-start(bf16[256,1024]{1,0:T(8,128)(2,1)S(1)} %place.1.refs_0_), channel_id=1, source_target_pairs={{0,8},{8,0},{16,24},{24,16},{1,9},{9,1},{17,25},{25,17},{2,10},{10... | collective-permute-start | bytes 1572872 | tf_op jit(solution)/shard_map/ppermute | solution.py:345
  56.9 9.6 %collective-permute-start.9 = (bf16[256,1024]{1,0:T(8,128)(2,1)S(1)}, bf16[256,1024]{1,0:T(8,128)(2,1)S(1)}, u32[]{:S(2)}, u32[]{:S(2)}) collective-permute-start(bf16[256,1024]{1,0:T(8,128)(2,1)S(1)} %collective-permute-done.7.refs_1_), channel_id=1, source_target_pairs={{0,8},{8,0},{16,24},{24,16},{1,9},{9,1},{17,25},{25,17},{2,10},{10... | collective-permute-start | bytes 1572872 | tf_op jit(solution)/shard_map/ppermute | solution.py:345
